TPU v7x, 32 devices: a whole 2x2x4 slice. The times are simulated.
32 devices in a mesh: dp: 16 (over z, y, core), fsdp: 2 (over x).
Axes of the slice: x: 2, y: 2, z: 4, core: 2. Of those that a mesh axis runs over, the one named last changes fastest.
Arguments:
- tokens: bfloat16 [64, 512, 1536], P(('dp', 'fsdp')), may hold values from -6 to 6
- cotangent: bfloat16 [64, 512, 1536], P(('dp', 'fsdp')), may hold values from -6 to 6
- lengths: int32 [64], replicated, may hold values from 1 to 512, as said below
- balance: int32 [64], replicated, may hold values from 0 to 63, as said below
- norm_gain: float32 [1536], P(('dp', 'fsdp')), may hold values from 0.5 to 1.5
- in_weight: float32 [1536, 6448], P(('dp', 'fsdp')), may hold values from -0.15625 to 0.15625
- conv_weight: float32 [3328, 4], P(('dp', 'fsdp')), may hold values from -3 to 3
- conv_bias: float32 [3328], P(('dp', 'fsdp')), may hold values from -3 to 3
- step_bias: float32 [48], replicated, may hold values from -6.9 to -2.3
- decay_log: float32 [48], replicated, may hold values from 0 to 2.77
- skip_weight: float32 [48], replicated, may hold values from 0.5 to 1.5
- inner_gain: float32 [3072], P(('dp', 'fsdp')), may hold values from 0.5 to 1.5
- out_weight: float32 [3072, 1536], P(('dp', 'fsdp')), may hold values from -0.109375 to 0.109375
Outputs:
- output: bfloat16 [64, 512, 1536], P(('dp', 'fsdp'))
- input_grad: bfloat16 [64, 512, 1536], P(('dp', 'fsdp'))
- grad_norm_gain: float32 [1536], P(('dp', 'fsdp'))
- grad_in_weight: float32 [1536, 6448], P(('dp', 'fsdp'))
- grad_conv_weight: float32 [3328, 4], P(('dp', 'fsdp'))
- grad_conv_bias: float32 [3328], P(('dp', 'fsdp'))
- grad_step_bias: float32 [48], replicated
- grad_decay_log: float32 [48], replicated
- grad_skip_weight: float32 [48], replicated
- grad_inner_gain: float32 [3072], P(('dp', 'fsdp'))
- grad_out_weight: float32 [3072, 1536], P(('dp', 'fsdp'))
Inputs may be any that keep to these rules, and one draw needn't show every extreme that they name: `lengths`: the longest slot has exactly 512 live positions. `balance`: a permutation; balanced slots 2d and 2d+1 stand on device d of the flat dp+fsdp order; balanced slot 2d is one of device d's own two loader slots, and balanced slot 2d+1 is the loader slot that device d's partner on dp (dp index differing in its lowest bit, same fsdp index) does not keep.
All inputs are finite; a program needn't handle non-finite values.
Results may differ from a plain program's by a relative error of at most 0.012.
Values may be sent and summed in bfloat16 or wider, within the bound.
A program may use at most 384 MiB of HBM per device.

v0:
```python
import functools
import jax
import jax.numpy as jnp
from jax import lax
from jax.experimental import pallas as pl
from jax.experimental.pallas import tpu as pltpu
from jax.sharding import PartitionSpec as P

D = 1536
INNER = 3072
HEADS = 48
HEADDIM = 64
STATE = 128
CONV = 4
XBC = 3328
PROJ = 6448
XE = XBC + 128
Q = 128
PAIRS = HEADS // 2

f32 = jnp.float32
bf16 = jnp.bfloat16
epsilon = 1e-05
AXES = ("dp", "fsdp")


def sigmoid(v):
    return 0.5 * jnp.tanh(0.5 * v) + 0.5


def dot_nn(a, b, precision=None):
    return jnp.dot(a, b, preferred_element_type=f32, precision=precision)


def dot_nt(a, b):
    return lax.dot_general(a, b, (((1,), (1,)), ((), ())), preferred_element_type=f32)


def dot_tn(a, b):
    return lax.dot_general(a, b, (((0,), (0,)), ((), ())), preferred_element_type=f32)


def lane_iota(shape):
    return lax.broadcasted_iota(jnp.int32, shape, len(shape) - 1)


def row_iota(shape):
    return lax.broadcasted_iota(jnp.int32, shape, len(shape) - 2)


H_UNIT = 48
H_TABLE = 4
O_UNIT = 32
O_TABLE = H_TABLE + D // H_UNIT


def source_chunk(meta, k, slot_chunks):
    return jnp.where(k < meta[1], k, k - meta[1] + slot_chunks)


def live_rows(meta, k):
    inside = k < meta[1]
    return jnp.where(inside, meta[2] - k * Q, meta[3] - (k - meta[1]) * Q)


def last_live(meta, k):
    return jnp.minimum(k, meta[0] - 1)


def last_padded(meta, k):
    return jnp.minimum(k, meta[0] + lax.rem(meta[0], 2) - 1)


def for_blocks(total, blocks, body):
    for b in range(blocks):
        pl.when(total >= 2 * b + 2)(functools.partial(body, b, 2 * Q))
        pl.when(total == 2 * b + 1)(functools.partial(body, b, Q))


def cost(flops, moved, transcendentals=0):
    return pl.CostEstimate(flops=int(flops), bytes_accessed=int(moved), transcendentals=int(transcendentals))


def params(**kw):
    return pltpu.CompilerParams(vmem_limit_bytes=60 * 1024 * 1024, **kw)


def project_kernel(slot_chunks, steps, tile, meta, u_ref, g_ref, w_ref, proj_ref, e_ref, ht_ref, h_ref):
    j = pl.program_id(0)
    total = meta[0]
    chunks = 2 * slot_chunks

    @pl.when(j == 0)
    def _():
        for k in range(chunks):

            @pl.when(k < total)
            def _():
                start = pl.multiple_of(source_chunk(meta, k, slot_chunks) * Q, Q)
                x = u_ref[pl.ds(start, Q), :].astype(f32)
                scale = lax.rsqrt(jnp.mean(x * x, axis=-1, keepdims=True) + epsilon)
                normed = x * scale * g_ref[...]
                h_ref[k * Q : (k + 1) * Q, :] = normed.astype(bf16)
                turned = normed.T.astype(bf16)
                for n in range(D // H_UNIT):
                    there = pl.ds(pl.multiple_of(meta[H_TABLE + n], 16), H_UNIT)
                    ht_ref[there, k * Q : (k + 1) * Q] = turned[n * H_UNIT : (n + 1) * H_UNIT, :]

            @pl.when(k >= total)
            def _():
                ht_ref[:, k * Q : (k + 1) * Q] = jnp.zeros((D, Q), bf16)

    edge = XBC + INNER - (steps - 1) * tile

    def block(b, rows):
        r = slice(b * 2 * Q, b * 2 * Q + rows)
        acc = dot_nn(h_ref[r, :], w_ref[...])
        proj_ref[r, :] = acc.astype(bf16)

        @pl.when(j == steps - 1)
        def _():
            tail = dot_nn(h_ref[r, :], w_ref[:, edge : edge + 128])
            e_ref[r, :] = jnp.where(lane_iota(tail.shape) < HEADS, tail, 0.0)

    for_blocks(total, chunks // 2, block)


def project(meta, u, g1, w1):
    rows = u.shape[0]
    tile = 512
    steps = pl.cdiv(PROJ, tile)
    return pl.pallas_call(
        functools.partial(project_kernel, rows // Q // 2, steps, tile),
        out_shape=(
            jax.ShapeDtypeStruct((rows, PROJ), bf16),
            jax.ShapeDtypeStruct((rows, 128), f32),
            jax.ShapeDtypeStruct((D, rows), bf16),
        ),
        grid_spec=pltpu.PrefetchScalarGridSpec(
            num_scalar_prefetch=1,
            grid=(steps,),
            in_specs=[
                pl.BlockSpec((rows, D), lambda j, m: (0, 0)),
                pl.BlockSpec((1, D), lambda j, m: (0, 0)),
                pl.BlockSpec((D, tile), lambda j, m: (0, j)),
            ],
            out_specs=[
                pl.BlockSpec((rows, tile), lambda j, m: (0, j)),
                pl.BlockSpec((rows, 128), lambda j, m: (0, 0)),
                pl.BlockSpec((D, rows), lambda j, m: (0, 0)),
            ],
            scratch_shapes=[pltpu.VMEM((rows, D), bf16)],
        ),
        compiler_params=params(),
        cost_estimate=cost(2 * rows * D * PROJ, 2 * (D * PROJ + rows * PROJ)),
        name="project",
    )(meta, u, g1, w1)


def conv_tile(buf, wc_ref, lanes):
    c = wc_ref[CONV : CONV + 1, lanes]
    for tap in range(CONV):
        c = c + wc_ref[tap : tap + 1, lanes] * buf[5 + tap : 5 + tap + Q, lanes]
    return c


def step_sizes(e_ref, par_ref):
    raw = e_ref[...] + par_ref[0:1, :]
    dt = jnp.maximum(raw, 0.0) + jnp.log1p(jnp.exp(-jnp.abs(raw)))
    decay = par_ref[1:2, :]
    lower = (row_iota((Q, Q)) >= lane_iota((Q, Q))).astype(f32)
    cum = dot_nn(lower, dt * decay, precision=lax.Precision.HIGHEST)
    return raw, dt, cum


def spread_heads(cum, dt, col_ref, dtp_ref):
    low = lane_iota((Q, 128)) < HEADDIM
    for p in range(PAIRS):
        for h in (2 * p, 2 * p + 1):
            col_ref[h] = jnp.broadcast_to(cum[:, h : h + 1], (Q, 128))
        dtp_ref[p] = jnp.where(
            low,
            jnp.broadcast_to(dt[:, 2 * p : 2 * p + 1], (Q, 128)),
            jnp.broadcast_to(dt[:, 2 * p + 1 : 2 * p + 2], (Q, 128)),
        )


def split_pair(v, low):
    zero = jnp.zeros_like(v)
    return jnp.concatenate([jnp.where(low, v, zero), jnp.where(low, zero, v)], axis=0)


def mixer_kernel(
    unroll, meta, proj_ref, e_ref, cot_ref, wc_ref, par_ref, skip_ref, g_ref,
    o_ref, ot_ref, y_ref, sin_ref, err_ref,
    buf, state, col_ref, dtp_ref, row_ref, q_ref,
):
    k = pl.program_id(0)
    total = meta[0]

    @pl.when((k == total) & (lax.rem(total, 2) == 1))
    def _():
        o_ref[...] = jnp.zeros_like(o_ref)
        ot_ref[...] = jnp.zeros_like(ot_ref)
        err_ref[...] = jnp.zeros_like(err_ref)

    @pl.when(k < total)
    def _():
        live = row_iota((Q, D)) < live_rows(meta, k)
        err_ref[...] = jnp.where(live, cot_ref[...].astype(f32), 0.0).astype(bf16)
        first = (k == 0) | (k == meta[1])

        @pl.when(first)
        def _():
            buf[0:8, :] = jnp.zeros((8, XBC), f32)
            state[...] = jnp.zeros_like(state)

        @pl.when(jnp.logical_not(first))
        def _():
            buf[0:8, :] = buf[Q : Q + 8, :]

        buf[8 : 8 + Q, :] = proj_ref[:, INNER : INNER + XBC].astype(f32)
        tail_lanes = slice(INNER, XBC)
        c = conv_tile(buf, wc_ref, tail_lanes)
        act = c * sigmoid(c)
        keys = act[:, :STATE]
        queries = act[:, STATE:].astype(bf16)
        keys_t = keys.T.astype(bf16)
        scores = dot_nn(queries, keys_t)
        _, dt, cum = step_sizes(e_ref, par_ref)
        row_ref[...] = cum.T
        spread_heads(cum, dt, col_ref, dtp_ref)
        lower = row_iota((Q, Q)) >= lane_iota((Q, Q))
        low = lane_iota((Q, 128)) < HEADDIM
        scores = jnp.where(lower, scores, 0.0)

        def pair(p):
            lanes = pl.ds(pl.multiple_of(p * 128, 128), 128)
            c = conv_tile(buf, wc_ref, lanes)
            values = c * sigmoid(c)
            col0, col1 = col_ref[2 * p], col_ref[2 * p + 1]
            both = jnp.where(low, col0, col1)
            end = both[Q - 1 : Q, :]
            stepped = values * dtp_ref[p]
            parts = split_pair(stepped.astype(bf16), low)
            mix = []
            for n, col in enumerate((col0, col1)):
                decay = jnp.exp(jnp.minimum(col - row_ref[pl.ds(2 * p + n, 1), :], 0.0))
                mix.append((scores * decay).astype(bf16))
            y = dot_nn(jnp.concatenate(mix, axis=1), parts)
            before = state[:, lanes]
            before_low = before.astype(bf16)
            sin_ref[0, :, lanes] = before_low
            y = y + dot_nn(queries, before_low) * jnp.exp(both)
            y = y + skip_ref[:, lanes] * values
            state[:, lanes] = before * jnp.exp(end) + dot_nn(
                keys_t, (stepped * jnp.exp(end - both)).astype(bf16)
            )
            z = proj_ref[:, lanes].astype(f32)
            gated = y * (z * sigmoid(z))
            y_ref[:, lanes] = y.astype(bf16)
            q_ref[:, lanes] = gated
            return gated * gated

        def body(i, squares):
            for n in range(unroll):
                squares = squares + pair(i * unroll + n)
            return squares

        squares = lax.fori_loop(0, PAIRS // unroll, body, jnp.zeros((Q, 128), f32))
        scale = lax.rsqrt(jnp.sum(squares, axis=-1, keepdims=True) / INNER + epsilon)

        def finish(p, _):
            lanes = pl.ds(pl.multiple_of(p * 128, 128), 128)
            out = q_ref[:, lanes] * scale * g_ref[:, lanes]
            o_ref[:, lanes] = out.astype(bf16)
            turned = out.T.astype(bf16)
            for n in range(128 // O_UNIT):
                there = pl.ds(pl.multiple_of(meta[O_TABLE + p * (128 // O_UNIT) + n], O_UNIT), O_UNIT)
                ot_ref[there, :] = turned[n * O_UNIT : (n + 1) * O_UNIT, :]
            return 0

        lax.fori_loop(0, PAIRS, finish, 0, unroll=2)


def mixer(meta, proj, e, cot, wc, par, skip, g2):
    rows = proj.shape[0]
    chunks = rows // Q
    const = lambda k, m: (0, 0)
    live = lambda k, m: (last_live(m, k), 0)
    return pl.pallas_call(
        functools.partial(mixer_kernel, 2),
        out_shape=(
            jax.ShapeDtypeStruct((rows, INNER), bf16),
            jax.ShapeDtypeStruct((INNER, rows), bf16),
            jax.ShapeDtypeStruct((rows, INNER), bf16),
            jax.ShapeDtypeStruct((chunks, STATE, INNER), bf16),
            jax.ShapeDtypeStruct((rows, D), bf16),
        ),
        grid_spec=pltpu.PrefetchScalarGridSpec(
            num_scalar_prefetch=1,
            grid=(chunks,),
            in_specs=[
                pl.BlockSpec((Q, PROJ), live),
                pl.BlockSpec((Q, 128), live),
                pl.BlockSpec((Q, D), lambda k, m: (source_chunk(m, last_live(m, k), chunks // 2), 0)),
                pl.BlockSpec((8, XBC), const),
                pl.BlockSpec((8, 128), const),
                pl.BlockSpec((1, INNER), const),
                pl.BlockSpec((1, INNER), const),
            ],
            out_specs=[
                pl.BlockSpec((Q, INNER), lambda k, m: (last_padded(m, k), 0)),
                pl.BlockSpec((INNER, Q), lambda k, m: (0, last_padded(m, k))),
                pl.BlockSpec((Q, INNER), live),
                pl.BlockSpec((1, STATE, INNER), lambda k, m: (last_live(m, k), 0, 0)),
                pl.BlockSpec((Q, D), lambda k, m: (last_padded(m, k), 0)),
            ],
            scratch_shapes=[
                pltpu.VMEM((Q + 8, XBC), f32),
                pltpu.VMEM((STATE, INNER), f32),
                pltpu.VMEM((HEADS, Q, 128), f32),
                pltpu.VMEM((PAIRS, Q, 128), f32),
                pltpu.VMEM((128, Q), f32),
                pltpu.VMEM((Q, INNER), f32),
            ],
        ),
        compiler_params=params(),
        cost_estimate=cost(chunks * PAIRS * 8 * 2 * Q * 128 * 128, 2 * rows * (PROJ + 3 * INNER)),
        name="mixer",
    )(meta, proj, e, cot, wc, par, skip, g2)


def gate_kernel(
    slot_chunks, meta, u_ref, err_ref, w_ref, o_ref, y_ref, z_ref, g_ref,
    out_ref, dy_ref, dz_ref, gi_ref,
    do_ref,
):
    b = pl.program_id(0)
    total = meta[0]

    @pl.when(b == 0)
    def _():
        out_ref[...] = jnp.zeros_like(out_ref)
        gi_ref[...] = jnp.zeros_like(gi_ref)

    def body(rows):
        halves = rows // Q
        if halves == 1:
            dz_ref[Q:, :] = jnp.zeros((Q, INNER), bf16)
        starts = []
        for n in range(halves):
            k = 2 * b + n
            start = pl.multiple_of(source_chunk(meta, k, slot_chunks) * Q, Q)
            starts.append(start)
        branch = dot_nn(o_ref[0:rows, :], w_ref[...])
        for n in range(halves):
            live = row_iota((Q, D)) < live_rows(meta, 2 * b + n)
            here = pl.ds(starts[n], Q)
            value = u_ref[here, :].astype(f32) + branch[n * Q : (n + 1) * Q, :]
            out_ref[here, :] = jnp.where(live, value, 0.0).astype(bf16)
        do_ref[0:rows, :] = dot_nt(err_ref[0:rows, :], w_ref[...])

        def sums(p, carry):
            squares, crossed = carry
            lanes = pl.ds(pl.multiple_of(p * 128, 128), 128)
            z = z_ref[0:rows, lanes].astype(f32)
            q = y_ref[0:rows, lanes].astype(f32) * (z * sigmoid(z))
            return squares + q * q, crossed + q * g_ref[:, lanes] * do_ref[0:rows, lanes]

        zero = jnp.zeros((rows, 128), f32)
        squares, crossed = lax.fori_loop(0, PAIRS, sums, (zero, zero), unroll=2)
        scale = lax.rsqrt(jnp.sum(squares, axis=-1, keepdims=True) / INNER + epsilon)
        factor = scale * scale * scale * (jnp.sum(crossed, axis=-1, keepdims=True) / INNER)

        def back(p, _):
            lanes = pl.ds(pl.multiple_of(p * 128, 128), 128)
            z = z_ref[0:rows, lanes].astype(f32)
            y = y_ref[0:rows, lanes].astype(f32)
            s = sigmoid(z)
            gate = z * s
            q = y * gate
            do = do_ref[0:rows, lanes]
            gi_ref[:, lanes] += jnp.sum(do * q * scale, axis=0, keepdims=True)
            dq = scale * (g_ref[:, lanes] * do) - q * factor
            dy_ref[0:rows, lanes] = (dq * gate).astype(bf16)
            dz_ref[0:rows, lanes] = (dq * y * (s * (1.0 + z * (1.0 - s)))).astype(bf16)
            return 0

        lax.fori_loop(0, PAIRS, back, 0, unroll=2)

    pl.when(total >= 2 * b + 2)(functools.partial(body, 2 * Q))
    pl.when(total == 2 * b + 1)(functools.partial(body, Q))


def last_block(m, b):
    return jnp.minimum(b, (m[0] + 1) // 2 - 1)


def gate(meta, u, err, w2, o, y, proj, g2):
    rows = u.shape[0]
    blocks = rows // (2 * Q)
    const = lambda b, m: (0, 0)
    live = lambda b, m: (last_block(m, b), 0)
    once = pl.Buffered(1)
    return pl.pallas_call(
        functools.partial(gate_kernel, rows // Q // 2),
        out_shape=(
            jax.ShapeDtypeStruct((rows, D), bf16),
            jax.ShapeDtypeStruct((rows, INNER), bf16),
            jax.ShapeDtypeStruct((rows, INNER), bf16),
            jax.ShapeDtypeStruct((1, INNER), f32),
        ),
        grid_spec=pltpu.PrefetchScalarGridSpec(
            num_scalar_prefetch=1,
            grid=(blocks,),
            in_specs=[
                pl.BlockSpec((rows, D), const, pipeline_mode=once),
                pl.BlockSpec((2 * Q, D), live),
                pl.BlockSpec((INNER, D), const, pipeline_mode=once),
                pl.BlockSpec((2 * Q, INNER), live),
                pl.BlockSpec((2 * Q, INNER), live),
                pl.BlockSpec((2 * Q, INNER), live),
                pl.BlockSpec((1, INNER), const),
            ],
            out_specs=[
                pl.BlockSpec((rows, D), const),
                pl.BlockSpec((2 * Q, INNER), live),
                pl.BlockSpec((2 * Q, INNER), live),
                pl.BlockSpec((1, INNER), const),
            ],
            scratch_shapes=[pltpu.VMEM((2 * Q, INNER), f32)],
        ),
        compiler_params=params(),
        cost_estimate=cost(4 * rows * D * INNER, 2 * (D * INNER + 5 * rows * INNER)),
        name="gate",
    )(meta, u, err, w2, o, y, proj, g2)


def back_kernel(
    unroll, part, parts, meta, x_ref, prev_ref, e_ref, dy_ref, sin_ref, wc_ref, par_ref, skip_ref, *rest
):
    carried, rest = (rest[:6], rest[6:]) if part > 0 else ((), rest)
    dx_ref, gconv_ref, gpar_ref, gskip_ref = rest[:4]
    passed_on, rest = (rest[4:6], rest[6:]) if part < parts - 1 else ((), rest[4:])
    buf, dbuf, dstate, col_ref, dtp_ref, row_ref, da_ref = rest
    i = pl.program_id(0)
    total = meta[0]
    begin, end = part_span(meta, part, parts)
    k = total - begin - i

    @pl.when(i == 0)
    def _():
        da_ref[...] = jnp.zeros_like(da_ref)
        if part == 0:
            gconv_ref[...] = jnp.zeros_like(gconv_ref)
            gpar_ref[...] = jnp.zeros_like(gpar_ref)
            gskip_ref[...] = jnp.zeros_like(gskip_ref)

            @pl.when(lax.rem(total, 2) == 1)
            def _():
                dx_ref[...] = jnp.zeros_like(dx_ref)

        else:
            for to, came in zip((gconv_ref, gpar_ref, gskip_ref, dstate), carried[1:5]):
                to[...] = came[...]
            dbuf[0:8, :] = carried[5][...]

    @pl.when((i >= 1) & (i <= end - begin))
    def _():
        first = (k == 0) | (k == meta[1])
        last = (k == total - 1) | (k == meta[1] - 1)

        @pl.when(first)
        def _():
            buf[0:8, :] = jnp.zeros((8, XBC), f32)

        @pl.when(jnp.logical_not(first))
        def _():
            buf[0:8, :] = prev_ref[8:16, INNER : INNER + XBC].astype(f32)

        @pl.when(last)
        def _():
            dbuf[Q : Q + 8, :] = jnp.zeros((8, XBC), f32)
            dstate[...] = jnp.zeros_like(dstate)

        @pl.when(jnp.logical_not(last))
        def _():
            dbuf[Q : Q + 8, :] = dbuf[0:8, :]

        buf[8 : 8 + Q, :] = x_ref[:, INNER : INNER + XBC].astype(f32)
        tail_lanes = slice(INNER, XBC)
        c_tail = conv_tile(buf, wc_ref, tail_lanes)
        s_tail = sigmoid(c_tail)
        act = c_tail * s_tail
        keys = act[:, :STATE].astype(bf16)
        queries = act[:, STATE:].astype(bf16)
        queries_t = act[:, STATE:].T.astype(bf16)
        scores = dot_nn(keys, queries_t)
        raw, dt, cum = step_sizes(e_ref, par_ref)
        row_ref[...] = cum.T
        spread_heads(cum, dt, col_ref, dtp_ref)
        upper = row_iota((Q, Q)) <= lane_iota((Q, Q))
        strict = row_iota((Q, Q)) < lane_iota((Q, Q))
        after = (row_iota((Q, Q)) >= lane_iota((Q, Q))).astype(bf16)
        low = lane_iota((Q, 128)) < HEADDIM
        scores = jnp.where(upper, scores, 0.0)
        half = (lax.broadcasted_iota(jnp.int32, (128, 128), 0) >= HEADDIM).astype(jnp.int32)
        head_lane = lane_iota((128, 128))

        def conv_back(lanes, dc):
            dbuf[0:Q, lanes] = dc
            dxbc = wc_ref[CONV - 1 : CONV, lanes] * dc
            for tap in range(CONV - 1):
                dxbc = dxbc + wc_ref[tap : tap + 1, lanes] * dbuf[3 - tap : 3 - tap + Q, lanes]
            dx_ref[:, lanes] = dxbc.astype(bf16)
            for tap in range(CONV):
                gconv_ref[tap : tap + 1, lanes] += jnp.sum(dc * buf[5 + tap : 5 + tap + Q, lanes], axis=0, keepdims=True)
            gconv_ref[CONV : CONV + 1, lanes] += jnp.sum(dc, axis=0, keepdims=True)

        def pair(p, carry):
            dscores, dquery, dkey, from_start, to_end, direct, thru = carry
            lanes = pl.ds(pl.multiple_of(p * 128, 128), 128)
            c = conv_tile(buf, wc_ref, lanes)
            s = sigmoid(c)
            values = c * s
            col0, col1 = col_ref[2 * p], col_ref[2 * p + 1]
            both = jnp.where(low, col0, col1)
            end = both[Q - 1 : Q, :]
            grown = jnp.exp(both)
            rest = jnp.exp(end - both)
            dtp = dtp_ref[p]
            stepped = values * dtp
            dy_low = dy_ref[:, lanes]
            dy = dy_low.astype(f32)
            parts = split_pair(dy_low, low)
            stepped_low = stepped.astype(bf16)
            dmix = dot_nt(stepped_low, parts)
            mix = []
            for n, col in enumerate((col0, col1)):
                decay = jnp.exp(jnp.minimum(row_ref[pl.ds(2 * p + n, 1), :] - col, 0.0))
                weighted = dmix[:, n * Q : (n + 1) * Q] * decay
                dscores = dscores + weighted
                mix.append((scores * decay).astype(bf16))
                passed = dot_nn((weighted * scores).astype(bf16), after)
                da_ref[pl.ds(2 * p + n, 1), :] = jnp.sum(jnp.where(strict, passed, 0.0), axis=0, keepdims=True)
            dstepped = dot_nn(jnp.concatenate(mix, axis=1), parts)
            dafter = dstate[:, lanes]
            dafter_low = dafter.astype(bf16)
            before_low = sin_ref[0, :, lanes]
            dend = dot_nn(keys, dafter_low) * rest
            grown_dy = (dy * grown).astype(bf16)
            select = (head_lane == 2 * p + half).astype(bf16)
            across = dot_nn(queries, before_low)
            from_start = from_start + dot_nn((across * grown * dy).astype(bf16), select)
            to_end = to_end + dot_nn((stepped * dend).astype(bf16), select)
            dstepped = dstepped + dend
            direct = direct + dot_nn((values * dstepped).astype(bf16), select)
            dquery = dquery + dot_nt(grown_dy, before_low)
            dkey = dkey + dot_nt((stepped * rest).astype(bf16), dafter_low)
            kept = jnp.exp(end) * dafter
            held = jnp.sum((kept * before_low.astype(f32)).reshape(8, 16, 128), axis=0)
            thru = thru + dot_nn(held.astype(bf16), select)
            dstate[:, lanes] = kept + dot_nn(queries_t, grown_dy)
            dvalues = dstepped * dtp + skip_ref[:, lanes] * dy
            gskip_ref[:, lanes] += jnp.sum(dy * values, axis=0, keepdims=True)
            conv_back(lanes, dvalues * (s * (1.0 + c * (1.0 - s))))
            return dscores, dquery, dkey, from_start, to_end, direct, thru

        def body(n, carry):
            for m in range(unroll):
                carry = pair(n * unroll + m, carry)
            return carry

        zero = jnp.zeros((Q, 128), f32)
        start = (zero,) * 6 + (jnp.zeros((16, 128), f32),)
        carry = lax.fori_loop(0, PAIRS // unroll, body, start)
        dscores, dquery, dkey, from_start, to_end, direct, thru = carry
        dscores = jnp.where(upper, dscores, 0.0)
        dkey = dkey + dot_nn(dscores.astype(bf16), queries)
        dquery = dquery + dot_nn(dscores.T.astype(bf16), keys)
        slope = s_tail * (1.0 + c_tail * (1.0 - s_tail))
        conv_back(slice(INNER, INNER + STATE), dkey * slope[:, :STATE])
        conv_back(slice(INNER + STATE, XBC), dquery * slope[:, STATE:])

        tail_sum = (row_iota((Q, Q)) <= lane_iota((Q, Q))).astype(f32)
        head_sum = (row_iota((Q, Q)) > lane_iota((Q, Q))).astype(f32)
        da = (
            da_ref[...].T
            + dot_nn(tail_sum, from_start, precision=lax.Precision.HIGHEST)
            + dot_nn(head_sum, to_end, precision=lax.Precision.HIGHEST)
            + jnp.sum(thru, axis=0, keepdims=True)
        )
        ddt = par_ref[1:2, :] * da + direct
        de = ddt * sigmoid(raw)
        de = jnp.where(lane_iota((Q, 128)) < HEADS, de, 0.0)
        dx_ref[:, XBC:] = de.astype(bf16)
        gpar_ref[0:1, :] += jnp.sum(de, axis=0, keepdims=True)
        gpar_ref[1:2, :] += jnp.sum(dt * da, axis=0, keepdims=True)

    if passed_on:

        @pl.when(i == pl.num_programs(0) - 1)
        def _():
            passed_on[0][...] = dstate[...]
            passed_on[1][...] = dbuf[0:8, :]


def part_span(meta, part, parts):
    return (meta[0] * part + parts - 1) // parts, (meta[0] * (part + 1) + parts - 1) // parts


def back(meta, part, parts, carried, proj, e, dy, sin, wc, par, skip):
    rows = proj.shape[0]
    chunks = rows // Q
    const = lambda i, m: (0, 0)

    def chunk(i, m):
        begin, end = part_span(m, part, parts)
        return jnp.clip(m[0] - begin - jnp.clip(i, 1, jnp.maximum(end - begin, 1)), 0, m[0] - 1)

    def written(i, m):
        begin, end = part_span(m, part, parts)
        block = jnp.where(end > begin, chunk(i, m), chunks)
        return jnp.where(i == 0, last_padded(m, m[0]), block) if part == 0 else block

    here = lambda i, m: (chunk(i, m), 0)
    out_shape = [
        jax.ShapeDtypeStruct((rows + Q, XE), bf16),
        jax.ShapeDtypeStruct((8, XBC), f32),
        jax.ShapeDtypeStruct((8, 128), f32),
        jax.ShapeDtypeStruct((1, INNER), f32),
    ]
    sums = [pl.BlockSpec((8, XBC), const), pl.BlockSpec((8, 128), const), pl.BlockSpec((1, INNER), const)]
    state = [pl.BlockSpec((STATE, INNER), const), pl.BlockSpec((8, XBC), const)]
    in_specs = [
        pl.BlockSpec((Q, PROJ), here),
        pl.BlockSpec((16, PROJ), lambda i, m: (jnp.maximum(chunk(i, m) * (Q // 16) - 1, 0), 0)),
        pl.BlockSpec((Q, 128), here),
        pl.BlockSpec((Q, INNER), here),
        pl.BlockSpec((1, STATE, INNER), lambda i, m: (chunk(i, m), 0, 0)),
        pl.BlockSpec((8, XBC), const),
        pl.BlockSpec((8, 128), const),
        pl.BlockSpec((1, INNER), const),
    ]
    out_specs = [pl.BlockSpec((Q, XE), lambda i, m: (written(i, m), 0))] + sums
    if part > 0:
        in_specs += [pl.BlockSpec(memory_space=pl.ANY)] + sums + state
    if part < parts - 1:
        out_shape += [jax.ShapeDtypeStruct((STATE, INNER), f32), jax.ShapeDtypeStruct((8, XBC), f32)]
        out_specs += state
    steps = -(-chunks // parts)
    return pl.pallas_call(
        functools.partial(back_kernel, 2, part, parts),
        out_shape=out_shape,
        grid_spec=pltpu.PrefetchScalarGridSpec(
            num_scalar_prefetch=1,
            grid=(steps + 1,),
            in_specs=in_specs,
            out_specs=out_specs,
            scratch_shapes=[
                pltpu.VMEM((Q + 8, XBC), f32),
                pltpu.VMEM((Q + 8, XBC), f32),
                pltpu.VMEM((STATE, INNER), f32),
                pltpu.VMEM((HEADS, Q, 128), f32),
                pltpu.VMEM((PAIRS, Q, 128), f32),
                pltpu.VMEM((128, Q), f32),
                pltpu.VMEM((128, Q), f32),
            ],
        ),
        input_output_aliases={9: 0} if part > 0 else {},
        compiler_params=params(),
        cost_estimate=cost(steps * PAIRS * 20 * 2 * Q * 128 * 128, 2 * steps * Q * (PROJ + 3 * INNER)),
        name="back",
    )(meta, proj, proj, e, dy, sin, wc, par, skip, *carried)


def weight_kernel(rows, swap_from, meta, at_ref, b_ref, mine_ref, other_ref):
    used = (meta[0] + 1) // 2
    half = at_ref.shape[0] // 2
    part_rows = half // 4
    swap = pl.program_id(0) >= swap_from

    def part(width):
        for c, out_ref in enumerate((mine_ref, other_ref)):

            def step(m, _):
                here = pl.ds(pl.multiple_of(c * half + 2 * m * part_rows, part_rows), 2 * part_rows)
                res = dot_nn(at_ref[here, 0:width], b_ref[0:width, :]).astype(bf16)
                for n in range(2):
                    place = jnp.where(swap, 2 * n + m, 2 * m + n)
                    there = pl.ds(pl.multiple_of(place * part_rows, part_rows), part_rows)
                    out_ref[there, :] = res[n * part_rows : (n + 1) * part_rows, :]
                return 0

            lax.fori_loop(0, 2, step, 0)

    for n in range(1, rows // (2 * Q) + 1):
        pl.when(used == n)(functools.partial(part, n * 2 * Q))


def weight_grad(meta, at, b, first, width, tile, swap_from):
    height, rows = at.shape
    offset = first // tile
    half = jax.ShapeDtypeStruct((height // 2, width), bf16)
    half_spec = pl.BlockSpec((height // 2, tile), lambda j, m: (0, j))
    return pl.pallas_call(
        functools.partial(weight_kernel, rows, swap_from),
        out_shape=(half, half),
        grid_spec=pltpu.PrefetchScalarGridSpec(
            num_scalar_prefetch=1,
            grid=(pl.cdiv(width, tile),),
            in_specs=[
                pl.BlockSpec((height, rows), lambda j, m: (0, 0)),
                pl.BlockSpec((rows, tile), lambda j, m: (0, j + offset)),
            ],
            out_specs=(half_spec, half_spec),
        ),
        compiler_params=params(),
        cost_estimate=cost(2 * rows * height * width, 2 * (rows * (height + width) + height * width)),
        name="weight_grad",
    )(meta, at, b)


def input_kernel(
    slot_chunks, steps, tile, meta, u_ref, err_ref, g_ref, dz_ref, dx_ref, w_ref, out0_ref, out1_ref, gn_ref, dh_ref
):
    j = pl.program_id(0)
    total = meta[0]
    chunks = 2 * slot_chunks
    last = w_ref[:, INNER + XBC : PROJ]
    cols = pl.ds(pl.multiple_of(j * tile, tile), tile)

    def block(b, rows):
        r = slice(b * 2 * Q, b * 2 * Q + rows)
        dh_ref[r, cols] = (
            dot_nt(dz_ref[r, :], w_ref[:, 0:INNER])
            + dot_nt(dx_ref[r, 0:XBC], w_ref[:, INNER : INNER + XBC])
            + dot_nt(dx_ref[r, XBC : XBC + HEADS], last)
        )

    for_blocks(total, chunks // 2, block)

    @pl.when(j == steps - 1)
    def _():
        out0_ref[...] = jnp.zeros_like(out0_ref)
        out1_ref[...] = jnp.zeros_like(out1_ref)
        gn_ref[...] = jnp.zeros_like(gn_ref)
        for k in range(chunks):

            @pl.when(k < total)
            def _():
                start = pl.multiple_of(source_chunk(meta, k, slot_chunks) * Q, Q)
                u = u_ref[pl.ds(start, Q), :].astype(f32)
                err = err_ref[k * Q : (k + 1) * Q, :].astype(f32)
                scale = lax.rsqrt(jnp.mean(u * u, axis=-1, keepdims=True) + epsilon)
                dh = dh_ref[k * Q : (k + 1) * Q, :]
                gn_ref[...] += jnp.sum(dh * (u * scale), axis=0, keepdims=True)
                n = dh * g_ref[...]
                inner = jnp.mean(u * n, axis=-1, keepdims=True)
                du = (err + scale * n - u * (scale * scale * scale * inner)).astype(bf16)

                @pl.when(k < meta[1])
                def _():
                    out0_ref[pl.ds(start, Q), :] = du

                @pl.when(k >= meta[1])
                def _():
                    out1_ref[pl.ds(pl.multiple_of(start - slot_chunks * Q, Q), Q), :] = du


def input_grad_of(meta, u, err, g1, dz, dx, w1):
    rows = u.shape[0]
    tile = 256
    steps = D // tile
    const = lambda j, m: (0, 0)
    once = pl.Buffered(1)
    return pl.pallas_call(
        functools.partial(input_kernel, rows // Q // 2, steps, tile),
        out_shape=(
            jax.ShapeDtypeStruct((rows // 2, D), bf16),
            jax.ShapeDtypeStruct((rows // 2, D), bf16),
            jax.ShapeDtypeStruct((1, D), f32),
        ),
        grid_spec=pltpu.PrefetchScalarGridSpec(
            num_scalar_prefetch=1,
            grid=(steps,),
            in_specs=[
                pl.BlockSpec((rows, D), const, pipeline_mode=once),
                pl.BlockSpec((rows, D), const, pipeline_mode=once),
                pl.BlockSpec((1, D), const),
                pl.BlockSpec((rows, INNER), const, pipeline_mode=once),
                pl.BlockSpec((rows, XE), const, pipeline_mode=once),
                pl.BlockSpec((tile, w1.shape[1]), lambda j, m: (j, 0)),
            ],
            out_specs=[
                pl.BlockSpec((rows // 2, D), const),
                pl.BlockSpec((rows // 2, D), const),
                pl.BlockSpec((1, D), const),
            ],
            scratch_shapes=[pltpu.VMEM((rows, D), f32)],
        ),
        compiler_params=params(),
        cost_estimate=cost(2 * rows * D * PROJ, 2 * (D * PROJ + rows * PROJ)),
        name="input_grad",
    )(meta, u, err, g1, dz, dx, w1)


def partner(value, axis, bit):
    mask = 2**bit
    pairs = [(source, source ^ mask) for source in range(lax.axis_size(axis))]
    return lax.ppermute(value, axis, pairs)


def log2(size):
    return size.bit_length() - 1


def halving_order(swap):
    fsdp = [("fsdp", bit) for bit in range(log2(lax.axis_size("fsdp")))]
    near = [("dp", 1)]
    far = [("dp", bit) for bit in range(2, log2(lax.axis_size("dp")))]
    return [("dp", 0)] + (near + fsdp if swap else fsdp + near) + far


def flat_bit(axis, bit):
    return bit + (log2(lax.axis_size("fsdp")) if axis == "dp" else 0)


def kept_at(order, owner):
    away = owner ^ lax.axis_index(AXES)
    place = jnp.zeros_like(away)
    for axis, bit in order:
        place = 2 * place + ((away >> flat_bit(axis, bit)) & 1)
    return place


def owner_at(order, place):
    away = jnp.zeros_like(place)
    for n, (axis, bit) in enumerate(order):
        away = away + (((place >> (len(order) - 1 - n)) & 1) << flat_bit(axis, bit))
    return away ^ lax.axis_index(AXES)


class Term:
    def __init__(self, value):
        self.value = value


class Columns:
    def __init__(self, width, swap):
        self.order = halving_order(swap)
        self.width = width
        self.terms = []
        self.phase = 0

    def done(self):
        return self.phase == len(self.order)

    def sum(self, start, stop):
        return sum(term.value[start:stop, at : at + self.width].astype(f32) for term, at in self.terms)

    def halve(self):
        self.rows //= 2
        return self.sum(self.rows, 2 * self.rows).astype(bf16)


class Chain:
    def __init__(self, halves, columns, grouped):
        mine, other = halves
        self.columns = columns
        if not grouped:
            count = lax.axis_size(AXES)
            whole = jnp.concatenate([mine, other]).reshape(count, -1, mine.shape[1])
            parts = []
            at = 0
            for c in columns:
                parts.append(whole[:, :, at : at + c.width][owner_at(c.order, jnp.arange(count))])
                at += c.width
            mine, other = jnp.concatenate(parts, axis=2).reshape(2, -1, mine.shape[1])
        self.going = [(columns, other)]
        kept = Term(mine)
        at = 0
        for c in columns:
            c.rows = mine.shape[0]
            c.terms.append((kept, at))
            at += c.width

    def halve(self):
        groups = {}
        for c in self.columns:
            if not c.done() and all(c not in members for members, _ in self.going):
                groups.setdefault((c.order[c.phase], c.rows), []).append(c)
        for members in groups.values():
            sent = [c.halve() for c in members]
            self.going.append((members, jnp.concatenate(sent, axis=1) if len(sent) > 1 else sent[0]))

    def exchange(self):
        for members, sent in self.going:
            first = members[0]
            came = Term(partner(sent, *first.order[first.phase]))
            at = 0
            for c in members:
                c.terms.append((came, at))
                c.phase += 1
                at += c.width
        self.going = []

    def finish(self):
        while not all(c.done() for c in self.columns):
            self.halve()
            self.exchange()
        return [c.sum(0, c.rows) for c in self.columns]


def tick(token, chains, after):
    last = {id(c.terms[-1][0]): c.terms[-1][0] for chain in chains for c in chain.columns if c.phase > 0}
    if last:
        *came, _ = lax.optimization_barrier([term.value for term in last.values()] + [after])
        for term, value in zip(last.values(), came):
            term.value = value
    for chain in chains:
        chain.halve()
    sent = [value for chain in chains for _, value in chain.going]
    *sent, token = lax.optimization_barrier(sent + [token])
    for chain in chains:
        chain.going = [(members, sent.pop(0)) for members, _ in chain.going]
        chain.exchange()
    return token


W_COLS = 6528
W_CUT = 3328


def gather_kernel(
    count, inner, flag_ref, shard_ref, tile_ref, tokens_ref, w_ref, tiles_ref, u_ref,
    kept, given, send_sem, recv_sem, tile_send, tile_recv, own_sem, give_send, give_recv,
):
    me = lax.axis_index("dp") * inner + lax.axis_index("fsdp")
    height = shard_ref.shape[0]
    x, core, y = flat_bit("fsdp", 0), flat_bit("dp", 0), flat_bit("dp", 1)
    far = [flat_bit("dp", bit) for bit in range(2, log2(lax.axis_size("dp")))]
    ways = (far + [y, x, core], far + [x, y, core])
    spans = (pl.ds(0, W_CUT), pl.ds(W_CUT, W_COLS - W_CUT))

    def place(away):
        return pl.ds(pl.multiple_of(jnp.bitwise_xor(me, away) * height, height), height)

    def link(bit):
        other = jnp.bitwise_xor(me, 2**bit)
        return (other // inner, other % inner)

    def last_step(half, away):
        return max((n for n, bit in enumerate(ways[half]) if (away >> bit) & 1), default=-1)

    def send(half, away, bit):
        src = shard_ref.at[:, spans[half]] if away == 0 else w_ref.at[place(away), spans[half]]
        return pltpu.make_async_remote_copy(
            src_ref=src,
            dst_ref=w_ref.at[place(away), spans[half]],
            send_sem=send_sem.at[half, away ^ 2**bit],
            recv_sem=recv_sem.at[half, away ^ 2**bit],
            device_id=link(bit),
            device_id_type=pl.DeviceIdType.MESH,
        )

    def receive(half, away):
        block = w_ref.at[place(away), spans[half]]
        return pltpu.make_async_remote_copy(
            src_ref=block,
            dst_ref=block,
            send_sem=send_sem.at[half, away],
            recv_sem=recv_sem.at[half, away],
            device_id=link(ways[half][last_step(half, away)]),
            device_id_type=pl.DeviceIdType.MESH,
        )

    def send_on(half, away):
        sends = [send(half, away, bit) for bit in ways[half][last_step(half, away) + 1 :]]
        for one in sends:
            one.start()
        return sends

    def tile_copy(n):
        other = jnp.bitwise_xor(me, n)
        return pltpu.make_async_remote_copy(
            src_ref=tile_ref,
            dst_ref=tiles_ref.at[me],
            send_sem=tile_send.at[n],
            recv_sem=tile_recv.at[n],
            device_id=(other // inner, other % inner),
            device_id_type=pl.DeviceIdType.MESH,
        )

    def start_tile(n, _):
        tile_copy(n).start()
        return 0

    def wait_tile(n, _):
        tile_copy(n).wait()
        return 0

    started = []
    for step in range(len(ways[0])):
        for half in range(2):
            one = send(half, 0, ways[half][step])
            one.start()
            started.append(one)
    own = pltpu.make_async_copy(shard_ref, w_ref.at[place(0), :], own_sem.at[0])
    own.start()
    lax.fori_loop(1, count, start_tile, 0)
    tiles_ref[me] = tile_ref[...]

    second = jnp.broadcast_to(flag_ref[0, 0], (1, D)) == 1
    rows = kept.shape[0]

    def choose(n, _):
        r = pl.ds(pl.multiple_of(n * 64, 64), 64)
        zero, one = tokens_ref[0, r, :].astype(f32), tokens_ref[1, r, :].astype(f32)
        kept[r, :] = jnp.where(second, one, zero).astype(bf16)
        given[r, :] = jnp.where(second, zero, one).astype(bf16)
        return 0

    lax.fori_loop(0, rows // 64, choose, 0)

    blocks = [(half, away) for half in range(2) for away in range(1, count)]
    blocks.sort(key=lambda b: (b[1].bit_count(), last_step(*b), b[0]))
    tail = []
    for n, (half, away) in enumerate(blocks):
        receive(half, away).wait_recv()
        started += send_on(half, away)
        if n == 8:
            keep = pltpu.make_async_copy(kept, u_ref.at[pl.ds(0, rows), :], own_sem.at[1])
            give = pltpu.make_async_remote_copy(
                src_ref=given,
                dst_ref=u_ref.at[pl.ds(rows, rows), :],
                send_sem=give_send,
                recv_sem=give_recv,
                device_id=link(core),
                device_id_type=pl.DeviceIdType.MESH,
            )
            keep.start()
            give.start()
            tail = [keep, give]
    for one in started:
        one.wait_send()
    for one in tail:
        one.wait()
    own.wait()
    lax.fori_loop(1, count, wait_tile, 0)


def gather(flag, shard, tile, tokens):
    count = lax.axis_size(AXES)
    slot = tokens.shape[1]
    whole = pl.BlockSpec(memory_space=pltpu.VMEM)
    anywhere = pl.BlockSpec(memory_space=pl.ANY)
    dma = pltpu.SemaphoreType.DMA
    return pl.pallas_call(
        functools.partial(gather_kernel, count, lax.axis_size("fsdp")),
        out_shape=(
            jax.ShapeDtypeStruct((D, W_COLS), bf16),
            jax.ShapeDtypeStruct((count, 8, 128), f32),
            jax.ShapeDtypeStruct((2 * slot, D), bf16),
        ),
        in_specs=[pl.BlockSpec(memory_space=pltpu.SMEM), whole, whole, whole],
        out_specs=(anywhere, whole, anywhere),
        scratch_shapes=[
            pltpu.VMEM((slot, D), bf16),
            pltpu.VMEM((slot, D), bf16),
            dma((2, count)),
            dma((2, count)),
            dma((count,)),
            dma((count,)),
            dma((2,)),
            dma,
            dma,
        ],
        compiler_params=params(has_side_effects=True),
        cost_estimate=cost(1e6, 2 * D * W_COLS),
        name="gather",
    )(flag, shard, tile, tokens)


def sum_kernel(count, inner, sent_ref, out_ref, came, send_sem, recv_sem):
    me = lax.axis_index("dp") * inner + lax.axis_index("fsdp")

    def copy(n):
        other = jnp.bitwise_xor(me, n)
        return pltpu.make_async_remote_copy(
            src_ref=sent_ref.at[other],
            dst_ref=came.at[n],
            send_sem=send_sem.at[n],
            recv_sem=recv_sem.at[n],
            device_id=(other // inner, other % inner),
            device_id_type=pl.DeviceIdType.MESH,
        )

    def start(n, _):
        copy(n).start()
        return 0

    def add(n, total):
        copy(n).wait()
        return total + came[n]

    lax.fori_loop(1, count, start, 0)
    out_ref[...] = lax.fori_loop(1, count, add, sent_ref[me])


def sum_small(tiles):
    count = tiles.shape[0]
    whole = pl.BlockSpec(memory_space=pltpu.VMEM)
    return pl.pallas_call(
        functools.partial(sum_kernel, count, lax.axis_size("fsdp")),
        out_shape=jax.ShapeDtypeStruct(tiles.shape[1:], f32),
        in_specs=[whole],
        out_specs=whole,
        scratch_shapes=[
            pltpu.VMEM(tiles.shape, f32),
            pltpu.SemaphoreType.DMA((count,)),
            pltpu.SemaphoreType.DMA((count,)),
        ],
        compiler_params=pltpu.CompilerParams(has_side_effects=True),
        cost_estimate=cost(count * 1024, 8 * count * 1024),
        name="sum_small",
    )(tiles)


def on_device(
    tokens, cotangent, lengths, balance, norm_gain, in_weight, conv_weight, conv_bias,
    step_bias, decay_log, skip_weight, inner_gain, out_weight,
):
    device = lax.axis_index(AXES)
    count = lax.axis_size(AXES)
    slot = tokens.shape[1]
    rows = 2 * slot
    first_source = balance[2 * device]
    second_source = balance[2 * device + 1]
    keep_second = first_source - 2 * device == 1
    cot = cotangent.reshape(rows, D)
    lens = [lengths[first_source], lengths[second_source]]
    chunks = [(n + Q - 1) // Q for n in lens]
    grouped = D // count == H_UNIT
    h_units = jnp.arange(D // H_UNIT)
    o_units = jnp.arange(INNER // O_UNIT)
    if grouped:
        order = halving_order(False)
        each = INNER // count // O_UNIT
        h_units = kept_at(order, h_units)
        o_units = kept_at(order, o_units // each) * each + o_units % each
    meta = jnp.concatenate(
        [jnp.stack([chunks[0] + chunks[1], chunks[0], lens[0], lens[1]]), h_units * H_UNIT, o_units * O_UNIT]
    ).astype(jnp.int32)

    small = [norm_gain, conv_weight.reshape(-1), conv_bias, inner_gain]
    sizes = [v.shape[0] for v in small]
    packed = jnp.concatenate(small).astype(bf16)
    if grouped:
        tile = jnp.pad(packed.astype(f32), (0, 1024 - packed.shape[0])).reshape(8, 128)
        shard = jnp.pad(in_weight.astype(bf16), ((0, 0), (0, W_COLS - PROJ)))
        w1, packed, u = gather(keep_second.astype(jnp.int32).reshape(1, 1), shard, tile, tokens)
        packed = packed.reshape(count, -1)
    else:
        outgoing = jnp.where(keep_second, tokens[0], tokens[1])
        incoming = partner(outgoing, "dp", 0)
        u = jnp.concatenate([jnp.where(keep_second, tokens[1], tokens[0]), incoming], axis=0)
        w1 = lax.all_gather(in_weight.astype(bf16), AXES, axis=0, tiled=True)
        packed = lax.all_gather(packed[None, :], AXES, axis=0, tiled=True).astype(f32)
    cuts = [sum(sizes[:n]) for n in range(len(sizes) + 1)]
    norm_full, conv_full, bias_full, inner_full = (
        packed[:, cuts[n] : cuts[n + 1]].reshape(-1) for n in range(4)
    )
    w2_own, w1 = lax.optimization_barrier([out_weight.astype(bf16), w1])
    w2 = lax.all_gather(w2_own, AXES, axis=0, tiled=True)

    wc = jnp.concatenate([conv_full.reshape(XBC, CONV).T, bias_full[None], jnp.zeros((3, XBC), f32)])
    rate = -jnp.exp(decay_log)
    par = jnp.zeros((8, 128), f32).at[0, :HEADS].set(step_bias).at[1, :HEADS].set(rate)
    skip = jnp.repeat(skip_weight, HEADDIM)[None]
    g1 = norm_full[None]
    g2 = inner_full[None]

    proj, e, ht = project(meta, u, g1, w1)
    o, ot, y, sin, err = mixer(meta, proj, e, cot, wc, par, skip, g2)
    never = 1 << 20

    def both(width):
        return [Columns(width // 2, False), Columns(width // 2, True)]

    halves = weight_grad(meta, ot, err, 0, D, D // 2, 1 if grouped else never)
    c_out = Chain(halves, both(D), grouped)
    meta = tick(meta, [c_out], err)
    out, dy, dz, gi = gate(meta, u, err, w2, o, y, proj, g2)
    meta = tick(meta, [c_out], gi)
    halves = weight_grad(meta, ht, dz, 0, INNER, INNER // 4, 2 if grouped else never)
    c_z = Chain(halves, both(INNER), grouped)
    parts = 3
    carried = ()
    for part in range(parts):
        meta = tick(meta, [c_out, c_z] if part > 0 else [c_z], carried[2] if part > 0 else gi)
        carried = back(meta, part, parts, carried, proj, e, dy, sin, wc, par, skip)
    dx, gconv, gpar, gskip = carried
    meta = tick(meta, [c_out, c_z], gpar)
    cut = 1792
    halves = weight_grad(meta, ht, dx, 0, cut, cut // 2, never)
    c_x = Chain(halves, [Columns(cut, False)], grouped)
    meta = tick(meta, [c_z, c_x], halves[1])
    halves = weight_grad(meta, ht, dx, cut, XE - cut, cut // 2, 0 if grouped else never)
    c_x1 = Chain(halves, [Columns(XE - cut, True)], grouped)
    meta = tick(meta, [c_x, c_x1], halves[1])
    meta = tick(meta, [c_x1], c_x1.columns[0].terms[-1][0].value)
    c_x.columns += c_x1.columns
    kept_half, given_half, gn = input_grad_of(meta, u, err, g1, dz, dx, w1)
    heads = jnp.concatenate(
        [gpar[0, :HEADS], gpar[1, :HEADS] * rate, gskip.reshape(HEADS, HEADDIM).sum(axis=1)]
    )
    owned = [gconv[:CONV].T.reshape(count, -1), gconv[CONV].reshape(count, -1), gi.reshape(count, -1)]
    tiles = jnp.concatenate(owned + [jnp.broadcast_to(heads, (count, 3 * HEADS)), gn.reshape(count, -1)], axis=1)
    tiles = jnp.pad(tiles, ((0, 0), (0, 1024 - tiles.shape[1]))).reshape(count, 8, 128)
    tiles = tick(tiles, [c_out, c_z, c_x], gn)
    sums = sum_small(tiles).reshape(-1)
    grad_out = jnp.concatenate(c_out.finish(), axis=1)
    grad_in = jnp.concatenate(c_z.finish() + c_x.finish(), axis=1)[:, :PROJ]

    back_half = partner(given_half, "dp", 0)
    input_grad = jnp.stack(
        [jnp.where(keep_second, back_half, kept_half), jnp.where(keep_second, kept_half, back_half)]
    )
    ends = [sum(v.shape[1] for v in owned[:n]) for n in range(4)]
    grad_conv = sums[: ends[1]].reshape(-1, CONV)
    grad_bias = sums[ends[1] : ends[2]]
    grad_inner = sums[ends[2] : ends[3]]
    heads = sums[ends[3] : ends[3] + 3 * HEADS]
    grad_norm = sums[ends[3] + 3 * HEADS :][: sizes[0]]
    return (
        out.reshape(2, slot, D),
        input_grad,
        grad_norm,
        grad_in,
        grad_conv,
        grad_bias,
        heads[:HEADS],
        heads[HEADS : 2 * HEADS],
        heads[2 * HEADS :],
        grad_inner,
        grad_out,
    )


def solution(mesh):
    flat = P(AXES)
    rowed = P(AXES, None)
    slots = P(AXES, None, None)
    return jax.shard_map(
        on_device,
        mesh=mesh,
        in_specs=(slots, slots, P(), P(), flat, rowed, rowed, flat, P(), P(), P(), flat, rowed),
        out_specs=(slots, slots, flat, rowed, rowed, flat, P(), P(), P(), flat, rowed),
        check_vma=False,
    )
```

profile of v0, /device:TPU:0, one launch (start us, length us, event | category | flops | bytes accessed | tf_op | source)
XLA Modules:
  0.0 598.4 jit_solution(3830692250132619686)
XLA Ops:
  7.3 1.3 fusion.15
  9.3 1.4 convert_element_type.447
  11.0 0.7 convert_element_type.448
  11.7 0.9 pad.21.shard_ref
  13.3 108.5 %gather.1 = (bf16[1536,6528]{1,0:T(8,128)(2,1)}, f32[32,8,128]{2,1,0:T(8,128)}, bf16[1024,1536]{1,0:T(8,128)(2,1)}) custom-call(s32[1,1]{1,0:T(1,128)} %bitcast.6.flag_ref, bf16[48,6528]{1,0:T(8,128)(2,1)} %pad.21.shard_ref, f32[8,128]{1,0:T(8,128)} %fusion.8.tile_ref, bf16[2,512,1536]{2,1,0:T(8,128)(2,1)} %tokens_ref.1), custom_call_target="tpu_custom_call" | custom-call | flops 1000000 | bytes 20054016 | tf_op jit(solution)/shard_map/gather/pallas_call | solution.py:1060
  127.6 0.9 copy.34
  132.3 1.9 concatenate.44.meta
  135.0 30.1 %project.1 = (bf16[1024,6448]{1,0:T(8,128)(2,1)}, f32[1024,128]{1,0:T(8,128)}, bf16[1536,1024]{1,0:T(8,128)(2,1)}) custom-call(s32[132]{0:T(256)} %concatenate.44.meta, bf16[1024,1536]{1,0:T(8,128)(2,1)} %get-tuple-element.126.u_ref, f32[1,1536]{1,0:T(1,128)} %broadcast_in_dim_reshape.12.g_ref, bf16[1536,6528]{1,0:T(8,128)(2,1)} %get-tuple-element.129.w_ref), custom_call_target="tpu_custom_call" | custom-call | flops 20283654144 | bytes 33013760 | tf_op jit(solution)/shard_map/project/pallas_call | solution.py:132
  165.1 53.8 %mixer.1 = (bf16[1024,3072]{1,0:T(8,128)(2,1)}, bf16[3072,1024]{1,0:T(8,128)(2,1)}, bf16[1024,3072]{1,0:T(8,128)(2,1)}, bf16[8,128,3072]{2,1,0:T(8,128)(2,1)}, bf16[1024,1536]{1,0:T(8,128)(2,1)}) custom-call(s32[132]{0:T(256)} %concatenate.44.meta, bf16[1024,6448]{1,0:T(8,128)(2,1)} %get-tuple-element.130.proj_ref.z_ref.x_ref.prev_ref, ...), custom_call_target="tpu_custom_call" | custom-call | flops 6442450944 | bytes 32079872 | tf_op jit(solution)/shard_map/mixer/pallas_call | solution.py:291
  218.9 15.0 %weight_grad.4 = (bf16[1536,1536]{1,0:T(8,128)(2,1)}, bf16[1536,1536]{1,0:T(8,128)(2,1)}) custom-call(s32[132]{0:T(256)} %concatenate.44.meta, bf16[3072,1024]{1,0:T(8,128)(2,1)} %get-tuple-element.132.at_ref, bf16[1024,1536]{1,0:T(8,128)(2,1)} %get-tuple-element.133.b_ref.err_ref), custom_call_target="tpu_custom_call" | custom-call | flops 9663676416 | bytes 18874368 | tf_op jit(solution)/shard_map/weight_grad/pallas_call | solution.py:707
  234.4 43.2 %gate.1 = (bf16[1024,1536]{1,0:T(8,128)(2,1)}, bf16[1024,3072]{1,0:T(8,128)(2,1)}, bf16[1024,3072]{1,0:T(8,128)(2,1)}, f32[1,3072]{1,0:T(1,128)}) custom-call(s32[132]{0:T(256)} %concatenate.44.meta, bf16[1024,1536]{1,0:T(8,128)(2,1)} %get-tuple-element.126.u_ref, bf16[1024,1536]{1,0:T(8,128)(2,1)} %get-tuple-element.133.b_ref.err_ref, ...), custom_call_target="tpu_custom_call" | custom-call | flops 19327352832 | bytes 40894464 | tf_op jit(solution)/shard_map/gate/pallas_call | solution.py:406
  277.6 3.9 add_convert_fusion.4
  281.5 14.9 %weight_grad.5 = (bf16[768,3072]{1,0:T(8,128)(2,1)}, bf16[768,3072]{1,0:T(8,128)(2,1)}) custom-call(s32[132]{0:T(256)} %concatenate.44.meta, bf16[1536,1024]{1,0:T(8,128)(2,1)} %get-tuple-element.145.at_ref, bf16[1024,3072]{1,0:T(8,128)(2,1)} %get-tuple-element.146.b_ref.dz_ref), custom_call_target="tpu_custom_call" | custom-call | flops 9663676416 | bytes 18874368 | tf_op jit(solution)/shard_map/weight_grad/pallas_call | solution.py:707
  296.9 1.0 collective-permute-start.2
  297.9 40.0 %back.3 = (bf16[1152,3456]{1,0:T(8,128)(2,1)}, f32[8,3328]{1,0:T(8,128)}, f32[8,128]{1,0:T(8,128)}, f32[1,3072]{1,0:T(1,128)}, f32[128,3072]{1,0:T(8,128)}, /*index=5*/f32[8,3328]{1,0:T(8,128)}) custom-call(s32[132]{0:T(256)} %concatenate.44.meta, bf16[1024,6448]{1,0:T(8,128)(2,1)} %get-tuple-element.130.proj_ref.z_ref.x_ref.prev_ref, ...), custom_call_target="tpu_custom_call" | custom-call | flops 6039797760 | bytes 12029952 | tf_op jit(solution)/shard_map/back/pallas_call | solution.py:653
  337.9 3.9 add_convert_fusion.10
  341.9 3.7 add_convert_fusion.2
  346.1 2.1 collective-permute-start.7
  348.2 1.4 collective-permute-start.5
  349.6 40.4 %back.4 = (bf16[1152,3456]{1,0:T(8,128)(2,1)}, f32[8,3328]{1,0:T(8,128)}, f32[8,128]{1,0:T(8,128)}, f32[1,3072]{1,0:T(1,128)}, f32[128,3072]{1,0:T(8,128)}, /*index=5*/f32[8,3328]{1,0:T(8,128)}) custom-call(s32[132]{0:T(256)} %concatenate.44.meta, ...), custom_call_target="tpu_custom_call", output_to_operand_aliasing={{0}: (9, {})} | custom-call | flops 6039797760 | bytes 12029952 | tf_op jit(solution)/shard_map/back/pallas_call | solution.py:653
  390.1 2.2 add_convert_fusion.17
  392.3 0.9 pad_maximum_fusion.5
  393.2 3.2 add_convert_fusion.8
  396.4 2.6 collective-permute-start.10
  399.1 22.6 %back.5 = (bf16[1152,3456]{1,0:T(8,128)(2,1)}, f32[8,3328]{1,0:T(8,128)}, f32[8,128]{1,0:T(8,128)}, f32[1,3072]{1,0:T(1,128)}) custom-call(s32[132]{0:T(256)} %concatenate.44.meta, bf16[1024,6448]{1,0:T(8,128)(2,1)} %get-tuple-element.130.proj_ref.z_ref.x_ref.prev_ref, ...), custom_call_target="tpu_custom_call", output_to_operand_aliasing={{0}: (9, {})} | custom-call | flops 6039797760 | bytes 12029952 | tf_op jit(solution)/shard_map/back/pallas_call | solution.py:653
  421.8 1.5 add_convert_fusion.23
  423.2 0.7 pad_maximum_fusion.9
  424.0 1.8 add_convert_fusion.15
  425.8 2.1 collective-permute-start.11
  427.9 11.0 %weight_grad.6 = (bf16[768,1792]{1,0:T(8,128)(2,1)}, bf16[768,1792]{1,0:T(8,128)(2,1)}) custom-call(s32[132]{0:T(256)} %concatenate.44.meta, bf16[1536,1024]{1,0:T(8,128)(2,1)} %get-tuple-element.145.at_ref, bf16[1152,3456]{1,0:T(8,128)(2,1)} %get-tuple-element.189.b_ref.dx_ref), custom_call_target="tpu_custom_call" | custom-call | flops 5637144576 | bytes 12320768 | tf_op jit(solution)/shard_map/weight_grad/pallas_call | solution.py:707
  438.9 1.7 add_convert_fusion.21
  441.3 11.4 %weight_grad.7 = (bf16[768,1664]{1,0:T(8,128)(2,1)}, bf16[768,1664]{1,0:T(8,128)(2,1)}) custom-call(s32[132]{0:T(256)} %concatenate.44.meta, bf16[1536,1024]{1,0:T(8,128)(2,1)} %get-tuple-element.145.at_ref, bf16[1152,3456]{1,0:T(8,128)(2,1)} %get-tuple-element.189.b_ref.dx_ref), custom_call_target="tpu_custom_call" | custom-call | flops 5234491392 | bytes 11665408 | tf_op jit(solution)/shard_map/weight_grad/pallas_call | solution.py:707
  452.7 3.7 add_convert_fusion
  463.0 0.9 collective-permute-start.15
  463.9 2.0 collective-permute-start.16
  466.2 3.0 add_convert_fusion.1
  469.2 1.2 collective-permute-start.18
  470.4 33.2 %input_grad.1 = (bf16[512,1536]{1,0:T(8,128)(2,1)}, bf16[512,1536]{1,0:T(8,128)(2,1)}, f32[1,1536]{1,0:T(1,128)}) custom-call(s32[132]{0:T(256)} %concatenate.44.meta, bf16[1024,1536]{1,0:T(8,128)(2,1)} %get-tuple-element.126.u_ref, bf16[1024,1536]{1,0:T(8,128)(2,1)} %get-tuple-element.133.b_ref.err_ref, f32[1,1536]{1,0:T(1,128)} %broadcast_in_dim_reshape.12.g_ref, ...), custom_call_target="tpu_custom_call" | custom-call | flops 20283654144 | bytes 33013760 | tf_op jit(solution)/shard_map/input_grad/pallas_call | solution.py:778
  505.0 0.8 concatenate.52
  507.3 1.6 add_convert_fusion.6
  508.9 2.5 add_convert_fusion.7
  511.4 18.6 %sum_small.1 = f32[8,128]{1,0:T(8,128)} custom-call(f32[32,8,128]{2,1,0:T(8,128)} %bitcast.36), custom_call_target="tpu_custom_call" | custom-call | flops 32768 | bytes 262144 | tf_op jit(solution)/shard_map/sum_small/pallas_call | solution.py:1115
  530.0 1.5 slice.570
  531.5 1.3 slice.572
  532.8 1.3 slice.576
  534.0 1.5 collective-permute-start.19
  535.5 0.8 slice.610
  537.0 1.7 convert_add_fusion.3
  538.7 0.9 pad_maximum_fusion.7
  539.6 1.4 add_convert_fusion.13
  541.0 10.6 %collective-permute-done.19 = bf16[192,1792]{1,0:T(8,128)(2,1)} collective-permute-done((bf16[192,1792]{1,0:T(8,128)(2,1)S(1)}, bf16[192,1792]{1,0:T(8,128)(2,1)}, u32[]{:S(2)}, u32[]{:S(2)}) %collective-permute-start.19) | collective-permute-done | bytes 688160 | tf_op jit(solution)/shard_map/ppermute | solution.py:812
  551.6 1.4 add_convert_fusion.12
  553.0 1.6 collective-permute-start.21
  554.6 1.5 convert_add_fusion.5
  556.8 12.4 %collective-permute-done.21 = bf16[96,3456]{1,0:T(8,128)(2,1)S(1)} collective-permute-done((bf16[96,3456]{1,0:T(8,128)(2,1)S(1)}, bf16[96,3456]{1,0:T(8,128)(2,1)S(1)}, u32[]{:S(2)}, u32[]{:S(2)}) %collective-permute-start.21) | collective-permute-done | bytes 663584 | tf_op jit(solution)/shard_map/ppermute | solution.py:812
  569.1 1.2 add_convert_fusion.19
  570.4 1.2 add_convert_fusion.18
  571.6 1.2 collective-permute-start.22
  572.8 1.8 select_bitcast_fusion.1
  574.6 1.9 pad_maximum_fusion
  576.5 11.2 %collective-permute-done.22 = bf16[48,3456]{1,0:T(8,128)(2,1)S(1)} collective-permute-done((bf16[48,3456]{1,0:T(8,128)(2,1)S(1)}, bf16[48,3456]{1,0:T(8,128)(2,1)S(1)}, u32[]{:S(2)}, u32[]{:S(2)}) %collective-permute-start.22) | collective-permute-done | bytes 331808 | tf_op jit(solution)/shard_map/ppermute | solution.py:812
  587.8 1.3 convert_add_fusion.1
  589.0 1.2 convert_add_fusion
  590.3 1.1 pad_maximum_fusion.1
  (143 shorter events, 19.4 us)
Async XLA Ops:
  7.2 3.5 copy-start.23
  7.2 3.5 copy-start.24
  7.2 3.5 copy-start.20
  7.2 3.7 copy-start.25
  7.2 3.7 copy-start.10
  7.2 227.2 %all-gather.2.cloned.1.call-start = ((), (), s32[]{:S(2)}) async-start(), calls=%async_computation | async-start | bytes 9732096 | tf_op jit(solution)/shard_map/all_gather | solution.py:1176
  13.3 112.4 %copy-start.19 = (s32[64]{0:T(128)S(1)}, s32[64]{0:T(128)}, u32[]{:S(2)}) copy-start(s32[64]{0:T(128)} %param.19) | copy-start | bytes 772
  129.5 1.1 copy-start.21
  129.5 2.5 copy-start.22
  129.5 2.6 copy-start.26
  132.3 32.8 %copy-start.14 = (f32[8,128]{1,0:T(8,128)}, f32[8,128]{1,0:T(8,128)S(1)}, u32[]{:S(2)}) copy-start(f32[8,128]{1,0:T(8,128)S(1)} %scatter.9.par_ref) | copy-start | bytes 12292
  233.9 43.7 %collective-permute-start = (bf16[1536,1536]{1,0:T(8,128)(2,1)}, bf16[1536,1536]{1,0:T(8,128)(2,1)}, u32[]{:S(2)}, u32[]{:S(2)}) collective-permute-start(bf16[1536,1536]{1,0:T(8,128)(2,1)} %get-tuple-element.141), channel_id=1, source_target_pairs={{0,2},{2,0},{4,6},{6,4},{8,10},{10,8},{12,14},{14,12},{16,18},{18,... | collective-permute-start | bytes 14155784 | tf_op jit(solution)/shard_map/ppermute | solution.py:812
  296.4 41.5 %collective-permute-start.3 = (bf16[768,3072]{1,0:T(8,128)(2,1)}, bf16[768,3072]{1,0:T(8,128)(2,1)}, u32[]{:S(2)}, u32[]{:S(2)}) collective-permute-start(bf16[768,3072]{1,0:T(8,128)(2,1)} %get-tuple-element.151), channel_id=1, source_target_pairs={{0,2},{2,0},{4,6},{6,4},{8,10},{10,8},{12,14},{14,12},{16,18},{18,... | collective-permute-start | bytes 14155784 | tf_op jit(solution)/shard_map/ppermute | solution.py:812
  296.4 41.4 %collective-permute-start.1 = (bf16[768,768]{1,0:T(8,128)(2,1)}, bf16[768,768]{1,0:T(8,128)(2,1)S(1)}, u32[]{:S(2)}, u32[]{:S(2)}) collective-permute-start(bf16[768,768]{1,0:T(8,128)(2,1)} %get-tuple-element.148), channel_id=1, source_target_pairs={{0,1},{1,0},{2,3},{3,2},{4,5},{5,4},{6,7},{7,6},{8,9},{9,8},{10,11... | collective-permute-start | bytes 3538952 | tf_op jit(solution)/shard_map/ppermute | solution.py:812
  296.9 41.0 %collective-permute-start.2 = (bf16[768,768]{1,0:T(8,128)(2,1)S(1)}, bf16[768,768]{1,0:T(8,128)(2,1)S(1)}, u32[]{:S(2)}, u32[]{:S(2)}) collective-permute-start(bf16[768,768]{1,0:T(8,128)(2,1)S(1)} %get-tuple-element.149), channel_id=1, source_target_pairs={{0,4},{2,6},{4,0},{6,2},{8,12},{10,14},{12,8},{14,10},{16,20},{18,... | collective-permute-start | bytes 3538952 | tf_op jit(solution)/shard_map/ppermute | solution.py:812
  337.8 83.9 %copy-start.4 = (bf16[768,768]{1,0:T(8,128)(2,1)}, bf16[768,768]{1,0:T(8,128)(2,1)S(1)}, u32[]{:S(2)}) copy-start(bf16[768,768]{1,0:T(8,128)(2,1)S(1)} %collective-permute-done.1) | copy-start | bytes 3538948
  337.9 83.9 %copy-start.5 = (bf16[768,768]{1,0:T(8,128)(2,1)}, bf16[768,768]{1,0:T(8,128)(2,1)S(1)}, u32[]{:S(2)}) copy-start(bf16[768,768]{1,0:T(8,128)(2,1)S(1)} %collective-permute-done.2) | copy-start | bytes 3538948
  337.9 4.0 copy-start
  345.6 44.5 %collective-permute-start.6 = (bf16[384,1536]{1,0:T(8,128)(2,1)}, bf16[384,1536]{1,0:T(8,128)(2,1)S(1)}, u32[]{:S(2)}, u32[]{:S(2)}) collective-permute-start(bf16[384,1536]{1,0:T(8,128)(2,1)} %get-tuple-element.161), channel_id=1, source_target_pairs={{0,1},{1,0},{2,3},{3,2},{4,5},{5,4},{6,7},{7,6},{8,9},{9,8},{10,11... | collective-permute-start | bytes 3538952 | tf_op jit(solution)/shard_map/ppermute | solution.py:812
  346.1 44.0 %collective-permute-start.7 = (bf16[384,1536]{1,0:T(8,128)(2,1)}, bf16[384,1536]{1,0:T(8,128)(2,1)}, u32[]{:S(2)}, u32[]{:S(2)}) collective-permute-start(bf16[384,1536]{1,0:T(8,128)(2,1)} %get-tuple-element.162), channel_id=1, source_target_pairs={{0,4},{2,6},{4,0},{6,2},{8,12},{10,14},{12,8},{14,10},{16,20},{18,... | collective-permute-start | bytes 3538952 | tf_op jit(solution)/shard_map/ppermute | solution.py:812
  348.2 41.9 %collective-permute-start.4 = (bf16[384,768]{1,0:T(8,128)(2,1)}, bf16[384,768]{1,0:T(8,128)(2,1)S(1)}, u32[]{:S(2)}, u32[]{:S(2)}) collective-permute-start(bf16[384,768]{1,0:T(8,128)(2,1)} %get-tuple-element.159), channel_id=1, source_target_pairs={{0,4},{2,6},{4,0},{6,2},{8,12},{10,14},{12,8},{14,10},{16,20},{18,... | collective-permute-start | bytes 1769480 | tf_op jit(solution)/shard_map/ppermute | solution.py:812
  348.2 41.9 %collective-permute-start.5 = (bf16[384,768]{1,0:T(8,128)(2,1)}, bf16[384,768]{1,0:T(8,128)(2,1)}, u32[]{:S(2)}, u32[]{:S(2)}) collective-permute-start(bf16[384,768]{1,0:T(8,128)(2,1)} %get-tuple-element.160), channel_id=1, source_target_pairs={{0,1},{1,0},{2,3},{3,2},{4,5},{5,4},{6,7},{7,6},{8,9},{9,8},{10,11... | collective-permute-start | bytes 1769480 | tf_op jit(solution)/shard_map/ppermute | solution.py:812
  390.0 31.7 %copy-start.7 = (bf16[384,768]{1,0:T(8,128)(2,1)}, bf16[384,768]{1,0:T(8,128)(2,1)S(1)}, u32[]{:S(2)}) copy-start(bf16[384,768]{1,0:T(8,128)(2,1)S(1)} %collective-permute-done.4) | copy-start | bytes 1769476
  390.1 48.8 %copy-start.6 = (bf16[384,1536]{1,0:T(8,128)(2,1)}, bf16[384,1536]{1,0:T(8,128)(2,1)S(1)}, u32[]{:S(2)}) copy-start(bf16[384,1536]{1,0:T(8,128)(2,1)S(1)} %collective-permute-done.6) | copy-start | bytes 3538948
  396.4 25.3 %collective-permute-start.8 = (bf16[192,1536]{1,0:T(8,128)(2,1)}, bf16[192,1536]{1,0:T(8,128)(2,1)}, u32[]{:S(2)}, u32[]{:S(2)}) collective-permute-start(bf16[192,1536]{1,0:T(8,128)(2,1)} %pad_maximum_fusion.5), channel_id=1, source_target_pairs={{0,8},{2,10},{4,12},{6,14},{8,0},{10,2},{12,4},{14,6},{16,24},{18,... | collective-permute-start | bytes 1769480 | tf_op jit(solution)/shard_map/ppermute | solution.py:812
  396.4 25.3 %collective-permute-start.9 = (bf16[192,1536]{1,0:T(8,128)(2,1)}, bf16[192,1536]{1,0:T(8,128)(2,1)}, u32[]{:S(2)}, u32[]{:S(2)}) collective-permute-start(bf16[192,1536]{1,0:T(8,128)(2,1)} %get-tuple-element.175), channel_id=1, source_target_pairs={{0,4},{2,6},{4,0},{6,2},{8,12},{10,14},{12,8},{14,10},{16,20},{18,... | collective-permute-start | bytes 1769480 | tf_op jit(solution)/shard_map/ppermute | solution.py:812
  396.4 25.3 %collective-permute-start.10 = (bf16[192,1536]{1,0:T(8,128)(2,1)}, bf16[192,1536]{1,0:T(8,128)(2,1)}, u32[]{:S(2)}, u32[]{:S(2)}) collective-permute-start(bf16[192,1536]{1,0:T(8,128)(2,1)} %get-tuple-element.176), channel_id=1, source_target_pairs={{0,1},{1,0},{2,3},{3,2},{4,5},{5,4},{6,7},{7,6},{8,9},{9,8},{10,11... | collective-permute-start | bytes 1769480 | tf_op jit(solution)/shard_map/ppermute | solution.py:812
  425.8 13.1 %collective-permute-start.11 = (bf16[96,3072]{1,0:T(8,128)(2,1)S(1)}, bf16[96,3072]{1,0:T(8,128)(2,1)S(1)}, u32[]{:S(2)}, u32[]{:S(2)}) collective-permute-start(bf16[96,3072]{1,0:T(8,128)(2,1)S(1)} %pad_maximum_fusion.6), channel_id=1, source_target_pairs={{0,8},{2,10},{4,12},{6,14},{8,0},{10,2},{12,4},{14,6},{16,24},{18,... | collective-permute-start | bytes 1769480 | tf_op jit(solution)/shard_map/ppermute | solution.py:812
  438.9 1.7 copy-start.8
  441.3 11.4 %collective-permute-start.12 = (bf16[768,1792]{1,0:T(8,128)(2,1)}, bf16[768,1792]{1,0:T(8,128)(2,1)S(1)}, u32[]{:S(2)}, u32[]{:S(2)}) collective-permute-start(bf16[768,1792]{1,0:T(8,128)(2,1)} %get-tuple-element.195), channel_id=1, source_target_pairs={{0,2},{2,0},{4,6},{6,4},{8,10},{10,8},{12,14},{14,12},{16,18},{18,... | collective-permute-start | bytes 8257544 | tf_op jit(solution)/shard_map/ppermute | solution.py:812
  452.7 3.8 copy-start.1
  452.7 4.8 copy-start.17
  452.7 6.1 %copy-start.15 = (f32[8,3328]{1,0:T(8,128)S(1)}, f32[8,3328]{1,0:T(8,128)}, u32[]{:S(2)}) copy-start(f32[8,3328]{1,0:T(8,128)} %get-tuple-element.210) | copy-start | bytes 319492
  456.5 9.7 %collective-permute-start.13 = (bf16[768,1664]{1,0:T(8,128)(2,1)}, bf16[768,1664]{1,0:T(8,128)(2,1)}, u32[]{:S(2)}, u32[]{:S(2)}) collective-permute-start(bf16[768,1664]{1,0:T(8,128)(2,1)} %get-tuple-element.198), channel_id=1, source_target_pairs={{0,2},{2,0},{4,6},{6,4},{8,10},{10,8},{12,14},{14,12},{16,18},{18,... | collective-permute-start | bytes 7667720 | tf_op jit(solution)/shard_map/ppermute | solution.py:812
  458.9 1.8 copy-start.18
  458.9 3.3 copy-start.27
  463.0 43.5 %collective-permute-start.15 = (bf16[96,1536]{1,0:T(8,128)(2,1)}, bf16[96,1536]{1,0:T(8,128)(2,1)S(1)}, u32[]{:S(2)}, u32[]{:S(2)}) collective-permute-start(bf16[96,1536]{1,0:T(8,128)(2,1)} %pad_maximum_fusion.9), channel_id=1, source_target_pairs={{0,16},{2,18},{4,20},{6,22},{8,24},{10,26},{12,28},{14,30},{16,0},... | collective-permute-start | bytes 884744 | tf_op jit(solution)/shard_map/ppermute | solution.py:812
  463.9 42.6 %collective-permute-start.16 = (bf16[48,3072]{1,0:T(8,128)(2,1)}, bf16[48,3072]{1,0:T(8,128)(2,1)S(1)}, u32[]{:S(2)}, u32[]{:S(2)}) collective-permute-start(bf16[48,3072]{1,0:T(8,128)(2,1)} %pad_maximum_fusion.10), channel_id=1, source_target_pairs={{0,16},{2,18},{4,20},{6,22},{8,24},{10,26},{12,28},{14,30},{16,0},... | collective-permute-start | bytes 884744 | tf_op jit(solution)/shard_map/ppermute | solution.py:812
  465.9 40.6 %collective-permute-start.17 = (bf16[384,1792]{1,0:T(8,128)(2,1)}, bf16[384,1792]{1,0:T(8,128)(2,1)}, u32[]{:S(2)}, u32[]{:S(2)}) collective-permute-start(bf16[384,1792]{1,0:T(8,128)(2,1)} %add_convert_fusion), channel_id=1, source_target_pairs={{0,1},{1,0},{2,3},{3,2},{4,5},{5,4},{6,7},{7,6},{8,9},{9,8},{10,11... | collective-permute-start | bytes 4128776 | tf_op jit(solution)/shard_map/ppermute | solution.py:812
  469.2 38.1 %copy-start.2 = (bf16[768,1792]{1,0:T(8,128)(2,1)S(1)}, bf16[768,1792]{1,0:T(8,128)(2,1)}, u32[]{:S(2)}) copy-start(bf16[768,1792]{1,0:T(8,128)(2,1)} %copy-done.1) | copy-start | bytes 8257540
  469.2 38.1 %collective-permute-start.18 = (bf16[384,1664]{1,0:T(8,128)(2,1)}, bf16[384,1664]{1,0:T(8,128)(2,1)}, u32[]{:S(2)}, u32[]{:S(2)}) collective-permute-start(bf16[384,1664]{1,0:T(8,128)(2,1)} %add_convert_fusion.1), channel_id=1, source_target_pairs={{0,4},{2,6},{4,0},{6,2},{8,12},{10,14},{12,8},{14,10},{16,20},{18,... | collective-permute-start | bytes 3833864 | tf_op jit(solution)/shard_map/ppermute | solution.py:812
  506.5 0.7 copy-start.13
  506.5 0.8 copy-start.11
  511.4 28.1 %collective-permute-start.20 = (bf16[192,1664]{1,0:T(8,128)(2,1)}, bf16[192,1664]{1,0:T(8,128)(2,1)}, u32[]{:S(2)}, u32[]{:S(2)}) collective-permute-start(bf16[192,1664]{1,0:T(8,128)(2,1)} %add_convert_fusion.7), channel_id=1, source_target_pairs={{0,1},{1,0},{2,3},{3,2},{4,5},{5,4},{6,7},{7,6},{8,9},{9,8},{10,11... | collective-permute-start | bytes 1916936 | tf_op jit(solution)/shard_map/ppermute | solution.py:812
  511.4 61.3 %collective-permute-start.14 = (bf16[512,1536]{1,0:T(8,128)(2,1)}, bf16[512,1536]{1,0:T(8,128)(2,1)}, u32[]{:S(2)}, u32[]{:S(2)}) collective-permute-start(bf16[512,1536]{1,0:T(8,128)(2,1)} %get-tuple-element.201), channel_id=1, source_target_pairs={{0,2},{2,0},{4,6},{6,4},{8,10},{10,8},{12,14},{14,12},{16,18},{18,... | collective-permute-start | bytes 4718600 | tf_op jit(solution)/shard_map/ppermute | solution.py:812
  534.0 17.5 %collective-permute-start.19 = (bf16[192,1792]{1,0:T(8,128)(2,1)S(1)}, bf16[192,1792]{1,0:T(8,128)(2,1)}, u32[]{:S(2)}, u32[]{:S(2)}) collective-permute-start(bf16[192,1792]{1,0:T(8,128)(2,1)S(1)} %add_convert_fusion.6), channel_id=1, source_target_pairs={{0,4},{2,6},{4,0},{6,2},{8,12},{10,14},{12,8},{14,10},{16,20},{18,... | collective-permute-start | bytes 2064392 | tf_op jit(solution)/shard_map/ppermute | solution.py:812
  541.0 13.6 %copy-start.9 = (bf16[96,3072]{1,0:T(8,128)(2,1)S(1)}, bf16[96,3072]{1,0:T(8,128)(2,1)}, u32[]{:S(2)}) copy-start(bf16[96,3072]{1,0:T(8,128)(2,1)} %copy-done.8) | copy-start | bytes 1769476
  541.0 13.6 %copy-start.12 = (bf16[48,3072]{1,0:T(8,128)(2,1)S(1)}, bf16[48,3072]{1,0:T(8,128)(2,1)}, u32[]{:S(2)}) copy-start(bf16[48,3072]{1,0:T(8,128)(2,1)} %copy-done.11) | copy-start | bytes 884740
  552.9 3.2 copy-start.16
  553.0 16.1 %collective-permute-start.21 = (bf16[96,3456]{1,0:T(8,128)(2,1)S(1)}, bf16[96,3456]{1,0:T(8,128)(2,1)S(1)}, u32[]{:S(2)}, u32[]{:S(2)}) collective-permute-start(bf16[96,3456]{1,0:T(8,128)(2,1)S(1)} %pad_maximum_fusion.4), channel_id=1, source_target_pairs={{0,8},{2,10},{4,12},{6,14},{8,0},{10,2},{12,4},{14,6},{16,24},{18,... | collective-permute-start | bytes 1990664 | tf_op jit(solution)/shard_map/ppermute | solution.py:812
  556.2 16.6 %copy-start.3 = (bf16[512,1536]{1,0:T(8,128)(2,1)S(1)}, bf16[512,1536]{1,0:T(8,128)(2,1)}, u32[]{:S(2)}) copy-start(bf16[512,1536]{1,0:T(8,128)(2,1)} %get-tuple-element.202) | copy-start | bytes 4718596
  571.6 16.2 %collective-permute-start.22 = (bf16[48,3456]{1,0:T(8,128)(2,1)S(1)}, bf16[48,3456]{1,0:T(8,128)(2,1)S(1)}, u32[]{:S(2)}, u32[]{:S(2)}) collective-permute-start(bf16[48,3456]{1,0:T(8,128)(2,1)S(1)} %pad_maximum_fusion.8), channel_id=1, source_target_pairs={{0,16},{2,18},{4,20},{6,22},{8,24},{10,26},{12,28},{14,30},{16,0},... | collective-permute-start | bytes 995336 | tf_op jit(solution)/shard_map/ppermute | solution.py:812
Sparse Core Ops, SparseCore 0:
  121.9 80.7 all-gather.1
where the time goes:
time: 608 us; the launch traced here: 598 us
  Pallas kernels  443 us (73%)
  other arithmetic  58.5 us (10%)
  waiting for transfers between devices  34.3 us (6%)
  local copies, waits for them, and re-layouts  22.6 us (4%)
  between operations  20.7 us (3%)
  starting transfers between devices  19.8 us (3%)
    pallas_call x1, Pallas kernels, gather(): pl.pallas_call(functools.partial(gather_kernel, count, lax.axis_size('fsd...  108 us
    pallas_call x3, Pallas kernels, back(): pl.pallas_call(functools.partial(back_kernel, 2, part, parts), out_shape=...  103 us
    pallas_call x1, Pallas kernels, mixer(): pl.pallas_call(functools.partial(mixer_kernel, 2), out_shape=(jax.ShapeDt...  53.8 us
    pallas_call x4, Pallas kernels, weight_grad(): pl.pallas_call(functools.partial(weight_kernel, rows, swap_from), out_sha...  52.3 us
    pallas_call x1, Pallas kernels, gate(): pl.pallas_call(functools.partial(gate_kernel, rows // Q // 2), out_shape=...  43.2 us
    convert_element_type x16, other arithmetic, halve(): return self.sum(self.rows, 2 * self.rows).astype(bf16)  38 us
    ppermute x23, waiting for transfers between devices, partner(): return lax.ppermute(value, axis, pairs)  34.2 us
    pallas_call x1, Pallas kernels, input_grad_of(): pl.pallas_call(functools.partial(input_kernel, rows // Q // 2, steps, til...  33.2 us
  transfers between devices with their start and end apart: 24, of which 3 were waited for; matrix products, arithmetic and copies ran while one was open for 7% of the time, Pallas kernels for 53%

commit v1 on v0

--- a/solution.py
+++ b/solution.py
@@ -1128,6 +1128,167 @@
     )(tiles)
 
 
+TILE_ROWS = 16
+X_CUT = 1792
+X_PIECES = tuple((which, 512 * n, width) for n in range(4) for which, width in ((0, 512 if n < 3 else 256), (1, 512 if n < 3 else 128)))
+
+
+def finish_kernel(
+    count, inner, m0, a0, b0, m1, a1, b1, gconv_ref, gpar_ref, par_ref, gskip_ref, gi_ref, gn_ref, given_ref,
+    x_ref, tile_ref, back_ref, *scratch,
+):
+    sources = ((m0, a0, b0), (m1, a1, b1))
+    terms, scratch = scratch[:2], scratch[2:]
+    sent, scratch = [scratch[2 * n : 2 * n + 2] for n in range(3)], scratch[6:]
+    came, scratch = [scratch[2 * n : 2 * n + 2] for n in range(3)], scratch[6:]
+    tiles, tiles_in, load_sem, send_sem, recv_sem, tile_send, tile_recv, give_send, give_recv = scratch
+    me = lax.axis_index("dp") * inner + lax.axis_index("fsdp")
+    far = [flat_bit("dp", bit) for bit in (2, 3)]
+    ways = ([flat_bit("dp", 1)] + far, [flat_bit("fsdp", 0)] + far)
+    tall = terms[0].shape[1]
+
+    def target(other):
+        return {"device_id": (other // inner, other % inner), "device_id_type": pl.DeviceIdType.MESH}
+
+    def load(n):
+        which, at, width = X_PIECES[n]
+        cols = pl.ds(at, width)
+        return [
+            pltpu.make_async_copy(ref.at[pl.ds(0, tall), cols], terms[which].at[i, :, cols], load_sem.at[n, i])
+            for i, ref in enumerate(sources[which])
+        ]
+
+    def copy(n, phase):
+        which, at, width = X_PIECES[n]
+        cols = pl.ds(at, width)
+        return pltpu.make_async_remote_copy(
+            src_ref=sent[phase][which].at[:, cols],
+            dst_ref=came[phase][which].at[:, cols],
+            send_sem=send_sem.at[n, phase],
+            recv_sem=recv_sem.at[n, phase],
+            **target(jnp.bitwise_xor(me, 2 ** ways[which][phase])),
+        )
+
+    def total(n, phase, start, rows):
+        which, at, width = X_PIECES[n]
+        parts = [terms[which][i, start : start + rows, at : at + width] for i in range(3)]
+        parts += [came[p][which][start : start + rows, at : at + width] for p in range(phase)]
+        return sum(part.astype(f32) for part in parts)
+
+    def go(n, phase):
+        which, at, width = X_PIECES[n]
+        rows = tall >> (phase + 1)
+        sent[phase][which][:, at : at + width] = total(n, phase, rows, rows).astype(bf16)
+        copy(n, phase).start()
+
+    def tile_copy(n):
+        other = jnp.bitwise_xor(me, n)
+        return pltpu.make_async_remote_copy(
+            src_ref=tiles.at[other],
+            dst_ref=tiles_in.at[n],
+            send_sem=tile_send.at[n],
+            recv_sem=tile_recv.at[n],
+            **target(other),
+        )
+
+    def start_tile(n, _):
+        tile_copy(n).start()
+        return 0
+
+    def add_tile(n, value):
+        tile_copy(n).wait()
+        return value + tiles_in[n]
+
+    give = pltpu.make_async_remote_copy(
+        src_ref=given_ref,
+        dst_ref=back_ref,
+        send_sem=give_send,
+        recv_sem=give_recv,
+        **target(jnp.bitwise_xor(me, 2 ** flat_bit("dp", 0))),
+    )
+    pieces = len(X_PIECES)
+    for n in range(pieces):
+        for one in load(n):
+            one.start()
+    for n in range(pieces):
+        for one in load(n):
+            one.wait()
+        go(n, 0)
+    give.start()
+
+    pick = lax.broadcasted_iota(jnp.int32, (INNER, 128), 0) // HEADDIM == lane_iota((INNER, 128))
+    skips = dot_nn(
+        jnp.broadcast_to(gskip_ref[...], (8, INNER)), pick.astype(f32), precision=lax.Precision.HIGHEST
+    )
+    tiles[...] = jnp.zeros_like(tiles)
+    for owner in range(count):
+        for row, ref in ((0, gconv_ref), (8, gi_ref), (9, gn_ref)):
+            each = ref.shape[1] // count
+            tiles[owner, row : row + ref.shape[0], 0:each] = ref[:, owner * each : (owner + 1) * each]
+        tiles[owner, 10:11, :] = gpar_ref[0:1, :]
+        tiles[owner, 11:12, :] = gpar_ref[1:2, :] * par_ref[1:2, :]
+        tiles[owner, 12:13, :] = skips[0:1, :]
+
+    lag = 2
+    for n in range(pieces + 2 * lag):
+        if n < pieces:
+            copy(n, 0).wait_recv()
+            go(n, 1)
+        if n == 1:
+            lax.fori_loop(1, count, start_tile, 0)
+        if lag <= n < pieces + lag:
+            copy(n - lag, 1).wait_recv()
+            go(n - lag, 2)
+        if n >= 2 * lag:
+            which, at, width = X_PIECES[n - 2 * lag]
+            copy(n - 2 * lag, 2).wait_recv()
+            x_ref[:, which * X_CUT + at : which * X_CUT + at + width] = total(n - 2 * lag, 3, 0, tall >> 3)
+    tile_ref[...] = lax.fori_loop(1, count, add_tile, tiles[me])
+    for n in range(pieces):
+        for phase in range(3):
+            copy(n, phase).wait_send()
+    give.wait()
+
+
+def finish(chains, gconv, gpar, par, gskip, gi, gn, given):
+    count = lax.axis_size(AXES)
+    operands = [term.value for chain in chains for term, _ in chain.columns[0].terms]
+    widths = [chain.columns[0].width for chain in chains]
+    tall = chains[0].columns[0].rows
+    dma = pltpu.SemaphoreType.DMA
+    anywhere = pl.BlockSpec(memory_space=pl.ANY)
+    whole = pl.BlockSpec(memory_space=pltpu.VMEM)
+    halves = [pltpu.VMEM((tall >> (phase + 1), width), bf16) for phase in range(3) for width in widths]
+    pieces = len(X_PIECES)
+    return pl.pallas_call(
+        functools.partial(finish_kernel, count, lax.axis_size("fsdp")),
+        out_shape=(
+            jax.ShapeDtypeStruct((tall >> 3, XE), f32),
+            jax.ShapeDtypeStruct((TILE_ROWS, 128), f32),
+            jax.ShapeDtypeStruct(given.shape, bf16),
+        ),
+        in_specs=[anywhere] * 6 + [whole] * 6 + [anywhere],
+        out_specs=(whole, whole, anywhere),
+        scratch_shapes=[
+            *(pltpu.VMEM((3, tall, width), bf16) for width in widths),
+            *halves,
+            *halves,
+            pltpu.VMEM((count, TILE_ROWS, 128), f32),
+            pltpu.VMEM((count, TILE_ROWS, 128), f32),
+            dma((pieces, 3)),
+            dma((pieces, 3)),
+            dma((pieces, 3)),
+            dma((count,)),
+            dma((count,)),
+            dma,
+            dma,
+        ],
+        compiler_params=params(has_side_effects=True),
+        cost_estimate=cost(1e7, 2e7),
+        name="finish",
+    )(*operands, gconv, gpar, par, gskip, gi, gn, given)
+
+
 def on_device(
     tokens, cotangent, lengths, balance, norm_gain, in_weight, conv_weight, conv_bias,
     step_bias, decay_log, skip_weight, inner_gain, out_weight,
@@ -1203,7 +1364,7 @@
         carried = back(meta, part, parts, carried, proj, e, dy, sin, wc, par, skip)
     dx, gconv, gpar, gskip = carried
     meta = tick(meta, [c_out, c_z], gpar)
-    cut = 1792
+    cut = X_CUT
     halves = weight_grad(meta, ht, dx, 0, cut, cut // 2, never)
     c_x = Chain(halves, [Columns(cut, False)], grouped)
     meta = tick(meta, [c_z, c_x], halves[1])
@@ -1211,29 +1372,38 @@
     c_x1 = Chain(halves, [Columns(XE - cut, True)], grouped)
     meta = tick(meta, [c_x, c_x1], halves[1])
     meta = tick(meta, [c_x1], c_x1.columns[0].terms[-1][0].value)
-    c_x.columns += c_x1.columns
     kept_half, given_half, gn = input_grad_of(meta, u, err, g1, dz, dx, w1)
-    heads = jnp.concatenate(
-        [gpar[0, :HEADS], gpar[1, :HEADS] * rate, gskip.reshape(HEADS, HEADDIM).sum(axis=1)]
-    )
-    owned = [gconv[:CONV].T.reshape(count, -1), gconv[CONV].reshape(count, -1), gi.reshape(count, -1)]
-    tiles = jnp.concatenate(owned + [jnp.broadcast_to(heads, (count, 3 * HEADS)), gn.reshape(count, -1)], axis=1)
-    tiles = jnp.pad(tiles, ((0, 0), (0, 1024 - tiles.shape[1]))).reshape(count, 8, 128)
-    tiles = tick(tiles, [c_out, c_z, c_x], gn)
-    sums = sum_small(tiles).reshape(-1)
+    conv_each = XBC // count
+    if grouped:
+        late = [chain.columns[0].terms[-1][0] for chain in (c_out, c_z)]
+        *came, gn = lax.optimization_barrier([term.value for term in late] + [gn])
+        for term, value in zip(late, came):
+            term.value = value
+        grad_x, tile, back_half = finish([c_x, c_x1], gconv, gpar, par, gskip, gi, gn, given_half)
+        grad_x = [grad_x]
+        grad_conv, grad_bias = tile[:CONV, :conv_each].T, tile[CONV, :conv_each]
+        grad_inner, grad_norm = tile[8, : sizes[3]], tile[9, : sizes[0]]
+        heads = [tile[10 + n, :HEADS] for n in range(3)]
+    else:
+        back_half = partner(given_half, "dp", 0)
+        heads = jnp.concatenate(
+            [gpar[0, :HEADS], gpar[1, :HEADS] * rate, gskip.reshape(HEADS, HEADDIM).sum(axis=1)]
+        )
+        owned = [gconv[:CONV].T.reshape(count, -1), gconv[CONV].reshape(count, -1), gi.reshape(count, -1)]
+        tiles = jnp.concatenate(owned + [jnp.broadcast_to(heads, (count, 3 * HEADS)), gn.reshape(count, -1)], axis=1)
+        tiles = jnp.pad(tiles, ((0, 0), (0, 1024 - tiles.shape[1]))).reshape(count, 8, 128)
+        sums = sum_small(tiles).reshape(-1)
+        grad_x = c_x.finish() + c_x1.finish()
+        ends = [sum(v.shape[1] for v in owned[:n]) for n in range(4)]
+        grad_conv = sums[: ends[1]].reshape(-1, CONV)
+        grad_bias = sums[ends[1] : ends[2]]
+        grad_inner = sums[ends[2] : ends[3]]
+        heads = sums[ends[3] : ends[3] + 3 * HEADS].reshape(3, HEADS)
+        grad_norm = sums[ends[3] + 3 * HEADS :][: sizes[0]]
     grad_out = jnp.concatenate(c_out.finish(), axis=1)
-    grad_in = jnp.concatenate(c_z.finish() + c_x.finish(), axis=1)[:, :PROJ]
-
-    back_half = partner(given_half, "dp", 0)
-    input_grad = jnp.stack(
-        [jnp.where(keep_second, back_half, kept_half), jnp.where(keep_second, kept_half, back_half)]
-    )
-    ends = [sum(v.shape[1] for v in owned[:n]) for n in range(4)]
-    grad_conv = sums[: ends[1]].reshape(-1, CONV)
-    grad_bias = sums[ends[1] : ends[2]]
-    grad_inner = sums[ends[2] : ends[3]]
-    heads = sums[ends[3] : ends[3] + 3 * HEADS]
-    grad_norm = sums[ends[3] + 3 * HEADS :][: sizes[0]]
+    grad_in = jnp.concatenate(c_z.finish() + grad_x, axis=1)[:, :PROJ]
+    swapped = [jnp.stack([back_half, kept_half]), jnp.stack([kept_half, back_half])]
+    input_grad = jnp.where(keep_second, *swapped)
     return (
         out.reshape(2, slot, D),
         input_grad,
@@ -1241,9 +1411,9 @@
         grad_in,
         grad_conv,
         grad_bias,
-        heads[:HEADS],
-        heads[HEADS : 2 * HEADS],
-        heads[2 * HEADS :],
+        heads[0],
+        heads[1],
+        heads[2],
         grad_inner,
         grad_out,
     )

time: 608 us -> 650 us (1.069)
  Pallas kernels: 443 us -> 554 us
  waiting for transfers between devices: 34.3 us -> 2.08 us
  other arithmetic: 58.5 us -> 40.1 us
  starting transfers between devices: 19.8 us -> 7.38 us
    pallas_call x3, Pallas kernels: 103 us -> 137 us  [back(): pl.pallas_call(functools.partial(back_kernel, 2, part, parts), out_shape=...]
    ppermute x23 -> x18, waiting for transfers between devices: 34.2 us -> 2.06 us  [partner(): return lax.ppermute(value, axis, pairs)]
    pallas_call x1, Pallas kernels: 18.6 us -> 42.8 us  [finish(): pl.pallas_call(functools.partial(finish_kernel, count, lax.axis_size('fsd...]
    pallas_call x1, Pallas kernels: 53.8 us -> 72.2 us  [mixer(): pl.pallas_call(functools.partial(mixer_kernel, 2), out_shape=(jax.ShapeDt...]
    convert_element_type x16 -> x10, other arithmetic: 38 us -> 24 us  [halve(): return self.sum(self.rows, 2 * self.rows).astype(bf16)]
    ppermute x23 -> x18, starting transfers between devices: 19.8 us -> 7.34 us  [partner(): return lax.ppermute(value, axis, pairs)]
    pallas_call x1, Pallas kernels: 43.2 us -> 55.4 us  [gate(): pl.pallas_call(functools.partial(gate_kernel, rows // Q // 2), out_shape=...]
    pallas_call x4, Pallas kernels: 52.3 us -> 60.3 us  [weight_grad(): pl.pallas_call(functools.partial(weight_kernel, rows, swap_from), out_sha...]
  transfers between devices with their start and end apart: 24 -> 19, of which waited for: 3 -> 1; matrix products, arithmetic and copies ran while one was open for 7% -> 2% of each run, Pallas kernels for 53% -> 60%
where the time goes in v1:
time: 650 us; the launch traced here: 641 us
  Pallas kernels  554 us (85%)
  other arithmetic  40.1 us (6%)
  between operations  20.6 us (3%)
  local copies, waits for them, and re-layouts  17 us (3%)
  starting transfers between devices  7.38 us (1%)
    pallas_call x3, Pallas kernels, back(): pl.pallas_call(functools.partial(back_kernel, 2, part, parts), out_shape=...  137 us
    pallas_call x1, Pallas kernels, gather(): pl.pallas_call(functools.partial(gather_kernel, count, lax.axis_size('fsd...  108 us
    pallas_call x1, Pallas kernels, mixer(): pl.pallas_call(functools.partial(mixer_kernel, 2), out_shape=(jax.ShapeDt...  72.2 us
    pallas_call x4, Pallas kernels, weight_grad(): pl.pallas_call(functools.partial(weight_kernel, rows, swap_from), out_sha...  60.3 us
    pallas_call x1, Pallas kernels, gate(): pl.pallas_call(functools.partial(gate_kernel, rows // Q // 2), out_shape=...  55.4 us
    pallas_call x1, Pallas kernels, finish(): pl.pallas_call(functools.partial(finish_kernel, count, lax.axis_size('fsd...  42.8 us
    pallas_call x1, Pallas kernels, input_grad_of(): pl.pallas_call(functools.partial(input_kernel, rows // Q // 2, steps, til...  40.2 us
    pallas_call x1, Pallas kernels, project(): pl.pallas_call(functools.partial(project_kernel, rows // Q // 2, steps, t...  37.2 us
  transfers between devices with their start and end apart: 19, of which 1 were waited for; matrix products, arithmetic and copies ran while one was open for 2% of the time, Pallas kernels for 60%

profile of v1, /device:TPU:0, one launch (start us, length us, event | category | flops | bytes accessed | tf_op | source)
XLA Modules:
  0.0 641.2 jit_solution(7593459660172533980)
XLA Ops:
  7.3 1.3 fusion.13
  9.3 1.4 convert_element_type.319
  10.7 0.1 copy.26
  10.8 0.1 reshape.110
  11.0 0.7 convert_element_type.320
  11.7 0.9 pad.17.shard_ref
  12.6 0.7 fusion.8.tile_ref
  13.3 108.5 %gather.1 = (bf16[1536,6528]{1,0:T(8,128)(2,1)}, f32[32,8,128]{2,1,0:T(8,128)}, bf16[1024,1536]{1,0:T(8,128)(2,1)}) custom-call(s32[1,1]{1,0:T(1,128)} %bitcast.6.flag_ref, bf16[48,6528]{1,0:T(8,128)(2,1)} %pad.17.shard_ref, f32[8,128]{1,0:T(8,128)} %fusion.8.tile_ref, bf16[2,512,1536]{2,1,0:T(8,128)(2,1)} %tokens_ref.1), custom_call_target="tpu_custom_call" | custom-call | flops 1000000 | bytes 20054016 | tf_op jit(solution)/shard_map/gather/pallas_call | solution.py:1060
  125.6 0.6 fusion.12
  127.6 0.9 copy.30
  128.6 0.1 slice.420
  128.7 0.1 slice.422
  128.7 0.7 broadcast_in_dim_reshape.12.g_ref
  129.4 0.1 broadcast_in_dim_reshape.13
  129.5 0.5 reshape_reshape.3
  130.1 0.5 copy.27
  130.6 0.7 broadcast_in_dim_reshape.14.skip_ref
  131.3 0.7 broadcast_in_dim_reshape.15.g_ref
  132.0 0.1 pad.38.clone
  132.1 0.2 scatter.9.par_ref
  132.3 1.9 concatenate.32.meta
  134.3 0.7 maximum_maximum_fusion.wc_ref
  135.0 37.2 %project.1 = (bf16[1024,6448]{1,0:T(8,128)(2,1)}, f32[1024,128]{1,0:T(8,128)}, bf16[1536,1024]{1,0:T(8,128)(2,1)}) custom-call(s32[132]{0:T(256)} %concatenate.32.meta, bf16[1024,1536]{1,0:T(8,128)(2,1)} %get-tuple-element.125.u_ref, f32[1,1536]{1,0:T(1,128)} %broadcast_in_dim_reshape.12.g_ref, bf16[1536,6528]{1,0:T(8,128)(2,1)} %get-tuple-element.128.w_ref), custom_call_target="tpu_custom_call" | custom-call | flops 20283654144 | bytes 33013760 | tf_op jit(solution)/shard_map/project/pallas_call | solution.py:132
  172.2 72.2 %mixer.1 = (bf16[1024,3072]{1,0:T(8,128)(2,1)}, bf16[3072,1024]{1,0:T(8,128)(2,1)}, bf16[1024,3072]{1,0:T(8,128)(2,1)}, bf16[8,128,3072]{2,1,0:T(8,128)(2,1)}, bf16[1024,1536]{1,0:T(8,128)(2,1)}) custom-call(s32[132]{0:T(256)} %concatenate.32.meta, bf16[1024,6448]{1,0:T(8,128)(2,1)} %get-tuple-element.129.proj_ref.z_ref.x_ref.prev_ref, ...), custom_call_target="tpu_custom_call" | custom-call | flops 6442450944 | bytes 32079872 | tf_op jit(solution)/shard_map/mixer/pallas_call | solution.py:291
  244.4 17.4 %weight_grad.4 = (bf16[1536,1536]{1,0:T(8,128)(2,1)}, bf16[1536,1536]{1,0:T(8,128)(2,1)}) custom-call(s32[132]{0:T(256)} %concatenate.32.meta, bf16[3072,1024]{1,0:T(8,128)(2,1)} %get-tuple-element.131.at_ref, bf16[1024,1536]{1,0:T(8,128)(2,1)} %get-tuple-element.132.b_ref.err_ref), custom_call_target="tpu_custom_call" | custom-call | flops 9663676416 | bytes 18874368 | tf_op jit(solution)/shard_map/weight_grad/pallas_call | solution.py:707
  261.7 55.4 %gate.1 = (bf16[1024,1536]{1,0:T(8,128)(2,1)}, bf16[1024,3072]{1,0:T(8,128)(2,1)}, bf16[1024,3072]{1,0:T(8,128)(2,1)}, f32[1,3072]{1,0:T(1,128)}) custom-call(s32[132]{0:T(256)} %concatenate.32.meta, bf16[1024,1536]{1,0:T(8,128)(2,1)} %get-tuple-element.125.u_ref, bf16[1024,1536]{1,0:T(8,128)(2,1)} %get-tuple-element.132.b_ref.err_ref, ...), custom_call_target="tpu_custom_call" | custom-call | flops 19327352832 | bytes 40894464 | tf_op jit(solution)/shard_map/gate/pallas_call | solution.py:406
  317.1 3.9 add_convert_fusion.4
  321.0 17.3 %weight_grad.5 = (bf16[768,3072]{1,0:T(8,128)(2,1)}, bf16[768,3072]{1,0:T(8,128)(2,1)}) custom-call(s32[132]{0:T(256)} %concatenate.32.meta, bf16[1536,1024]{1,0:T(8,128)(2,1)} %get-tuple-element.146.at_ref, bf16[1024,3072]{1,0:T(8,128)(2,1)} %get-tuple-element.147.b_ref.dz_ref), custom_call_target="tpu_custom_call" | custom-call | flops 9663676416 | bytes 18874368 | tf_op jit(solution)/shard_map/weight_grad/pallas_call | solution.py:707
  338.4 57.0 %back.3 = (bf16[1152,3456]{1,0:T(8,128)(2,1)}, f32[8,3328]{1,0:T(8,128)}, f32[8,128]{1,0:T(8,128)}, f32[1,3072]{1,0:T(1,128)}, f32[128,3072]{1,0:T(8,128)}, /*index=5*/f32[8,3328]{1,0:T(8,128)}) custom-call(s32[132]{0:T(256)} %concatenate.32.meta, bf16[1024,6448]{1,0:T(8,128)(2,1)} %get-tuple-element.129.proj_ref.z_ref.x_ref.prev_ref, ...), custom_call_target="tpu_custom_call" | custom-call | flops 6039797760 | bytes 12029952 | tf_op jit(solution)/shard_map/back/pallas_call | solution.py:653
  395.5 3.9 add_convert_fusion.8
  399.4 0.1 copy-done.3
  399.5 3.7 add_convert_fusion.2
  403.2 2.0 collective-permute-start.4
  405.2 2.0 collective-permute-start.5
  407.2 40.5 %back.4 = (bf16[1152,3456]{1,0:T(8,128)(2,1)}, f32[8,3328]{1,0:T(8,128)}, f32[8,128]{1,0:T(8,128)}, f32[1,3072]{1,0:T(1,128)}, f32[128,3072]{1,0:T(8,128)}, /*index=5*/f32[8,3328]{1,0:T(8,128)}) custom-call(s32[132]{0:T(256)} %concatenate.32.meta, ...), custom_call_target="tpu_custom_call", output_to_operand_aliasing={{0}: (9, {})} | custom-call | flops 6039797760 | bytes 12029952 | tf_op jit(solution)/shard_map/back/pallas_call | solution.py:653
  447.8 2.2 add_convert_fusion.13
  450.0 0.9 pad_maximum_fusion.2
  450.9 3.2 add_convert_fusion.6
  454.1 0.1 collective-permute-start.10
  454.2 40.0 %back.5 = (bf16[1152,3456]{1,0:T(8,128)(2,1)}, f32[8,3328]{1,0:T(8,128)}, f32[8,128]{1,0:T(8,128)}, f32[1,3072]{1,0:T(1,128)}) custom-call(s32[132]{0:T(256)} %concatenate.32.meta, bf16[1024,6448]{1,0:T(8,128)(2,1)} %get-tuple-element.129.proj_ref.z_ref.x_ref.prev_ref, ...), custom_call_target="tpu_custom_call", output_to_operand_aliasing={{0}: (9, {})} | custom-call | flops 6039797760 | bytes 12029952 | tf_op jit(solution)/shard_map/back/pallas_call | solution.py:653
  494.2 1.5 add_convert_fusion.17
  495.7 0.7 pad_maximum_fusion.5
  496.4 1.8 add_convert_fusion.11
  498.3 12.6 %weight_grad.6 = (bf16[768,1792]{1,0:T(8,128)(2,1)}, bf16[768,1792]{1,0:T(8,128)(2,1)}) custom-call(s32[132]{0:T(256)} %concatenate.32.meta, bf16[1536,1024]{1,0:T(8,128)(2,1)} %get-tuple-element.146.at_ref, bf16[1152,3456]{1,0:T(8,128)(2,1)} %get-tuple-element.187.b_ref.dx_ref), custom_call_target="tpu_custom_call" | custom-call | flops 5637144576 | bytes 12320768 | tf_op jit(solution)/shard_map/weight_grad/pallas_call | solution.py:707
  511.0 1.7 add_convert_fusion.15
  512.7 0.7 pad_maximum_fusion.6
  513.4 13.0 %weight_grad.7 = (bf16[768,1664]{1,0:T(8,128)(2,1)}, bf16[768,1664]{1,0:T(8,128)(2,1)}) custom-call(s32[132]{0:T(256)} %concatenate.32.meta, bf16[1536,1024]{1,0:T(8,128)(2,1)} %get-tuple-element.146.at_ref, bf16[1152,3456]{1,0:T(8,128)(2,1)} %get-tuple-element.187.b_ref.dx_ref), custom_call_target="tpu_custom_call" | custom-call | flops 5234491392 | bytes 11665408 | tf_op jit(solution)/shard_map/weight_grad/pallas_call | solution.py:707
  526.5 1.8 add_convert_fusion
  528.4 2.9 collective-permute-start.17
  531.4 2.0 collective-permute-done.14.a1
  533.4 0.3 add_convert_fusion.1
  533.7 1.1 copy-done.2
  534.8 40.2 %input_grad.1 = (bf16[512,1536]{1,0:T(8,128)(2,1)}, bf16[512,1536]{1,0:T(8,128)(2,1)}, f32[1,1536]{1,0:T(1,128)}) custom-call(s32[132]{0:T(256)} %concatenate.32.meta, bf16[1024,1536]{1,0:T(8,128)(2,1)} %get-tuple-element.125.u_ref, bf16[1024,1536]{1,0:T(8,128)(2,1)} %get-tuple-element.132.b_ref.err_ref, f32[1,1536]{1,0:T(1,128)} %broadcast_in_dim_reshape.12.g_ref, ...), custom_call_target="tpu_custom_call" | custom-call | flops 20283654144 | bytes 33013760 | tf_op jit(solution)/shard_map/input_grad/pallas_call | solution.py:778
  575.1 1.8 convert_add_fusion.1
  576.9 0.9 pad_maximum_fusion.4
  577.8 2.5 convert_add_fusion.3
  580.3 1.1 copy-done.5
  581.3 42.8 %finish.1 = (f32[48,3456]{1,0:T(8,128)}, f32[16,128]{1,0:T(8,128)}, bf16[512,1536]{1,0:T(8,128)(2,1)}) custom-call(bf16[768,1792]{1,0:T(8,128)(2,1)} %get-tuple-element.188.m0, bf16[768,1792]{1,0:T(8,128)(2,1)} %collective-permute-done.12.a0, bf16[384,1792]{1,0:T(8,128)(2,1)} %copy-done.5, bf16[768,1664]{1,0:T(8,128)(2,1)} %get-tuple-element.197.m1, ...), custom_call_target="tpu_custom_call" | custom-call | flops 10000000 | bytes 20000000 | tf_op jit(solution)/shard_map/finish/pallas_call | solution.py:1263
  624.2 1.4 slice_bitcast_fusion.2
  625.5 1.3 slice_bitcast_fusion
  626.8 1.2 slice_bitcast_fusion.5
  628.0 1.2 slice_bitcast_fusion.1
  629.2 3.8 maximum_select_fusion
  633.0 1.1 pad_maximum_fusion
  (94 shorter events, 0.8 us)
Async XLA Ops:
  7.2 3.5 copy-start.21
  7.2 3.5 copy-start.22
  7.2 3.5 copy-start.18
  7.2 3.7 copy-start.23
  7.2 3.7 copy-start.15
  7.2 254.5 %all-gather.2.cloned.1.call-start = ((), (), s32[]{:S(2)}) async-start(), calls=%async_computation | async-start | bytes 9732096 | tf_op jit(solution)/shard_map/all_gather | solution.py:1337
  13.3 112.4 %copy-start.17 = (s32[64]{0:T(128)S(1)}, s32[64]{0:T(128)}, u32[]{:S(2)}) copy-start(s32[64]{0:T(128)} %param.19) | copy-start | bytes 772
  129.5 1.1 copy-start.19
  129.5 2.5 copy-start.20
  129.5 2.6 copy-start.24
  132.3 39.9 %copy-start.16 = (f32[8,128]{1,0:T(8,128)}, f32[8,128]{1,0:T(8,128)S(1)}, u32[]{:S(2)}) copy-start(f32[8,128]{1,0:T(8,128)S(1)} %scatter.9.par_ref) | copy-start | bytes 12292
  261.7 55.4 %collective-permute-start = (bf16[1536,1536]{1,0:T(8,128)(2,1)}, bf16[1536,1536]{1,0:T(8,128)(2,1)}, u32[]{:S(2)}, u32[]{:S(2)}) collective-permute-start(bf16[1536,1536]{1,0:T(8,128)(2,1)} %get-tuple-element.140), channel_id=1, source_target_pairs={{0,2},{2,0},{4,6},{6,4},{8,10},{10,8},{12,14},{14,12},{16,18},{18,... | collective-permute-start | bytes 14155784 | tf_op jit(solution)/shard_map/ppermute | solution.py:812
  338.3 57.2 %collective-permute-start.3 = (bf16[768,3072]{1,0:T(8,128)(2,1)}, bf16[768,3072]{1,0:T(8,128)(2,1)}, u32[]{:S(2)}, u32[]{:S(2)}) collective-permute-start(bf16[768,3072]{1,0:T(8,128)(2,1)} %get-tuple-element.149), channel_id=1, source_target_pairs={{0,2},{2,0},{4,6},{6,4},{8,10},{10,8},{12,14},{14,12},{16,18},{18,... | collective-permute-start | bytes 14155784 | tf_op jit(solution)/shard_map/ppermute | solution.py:812
  338.3 57.1 %collective-permute-start.1 = (bf16[768,768]{1,0:T(8,128)(2,1)}, bf16[768,768]{1,0:T(8,128)(2,1)S(1)}, u32[]{:S(2)}, u32[]{:S(2)}) collective-permute-start(bf16[768,768]{1,0:T(8,128)(2,1)} %get-tuple-element.143), channel_id=1, source_target_pairs={{0,1},{1,0},{2,3},{3,2},{4,5},{5,4},{6,7},{7,6},{8,9},{9,8},{10,11... | collective-permute-start | bytes 3538952 | tf_op jit(solution)/shard_map/ppermute | solution.py:812
  338.3 57.1 %collective-permute-start.2 = (bf16[768,768]{1,0:T(8,128)(2,1)S(1)}, bf16[768,768]{1,0:T(8,128)(2,1)S(1)}, u32[]{:S(2)}, u32[]{:S(2)}) collective-permute-start(bf16[768,768]{1,0:T(8,128)(2,1)S(1)} %get-tuple-element.144), channel_id=1, source_target_pairs={{0,4},{2,6},{4,0},{6,2},{8,12},{10,14},{12,8},{14,10},{16,20},{18,... | collective-permute-start | bytes 3538952 | tf_op jit(solution)/shard_map/ppermute | solution.py:812
  395.4 98.8 %copy-start.6 = (bf16[768,768]{1,0:T(8,128)(2,1)}, bf16[768,768]{1,0:T(8,128)(2,1)S(1)}, u32[]{:S(2)}) copy-start(bf16[768,768]{1,0:T(8,128)(2,1)S(1)} %collective-permute-done.1) | copy-start | bytes 3538948
  395.4 98.8 %copy-start.7 = (bf16[768,768]{1,0:T(8,128)(2,1)}, bf16[768,768]{1,0:T(8,128)(2,1)S(1)}, u32[]{:S(2)}) copy-start(bf16[768,768]{1,0:T(8,128)(2,1)S(1)} %collective-permute-done.2) | copy-start | bytes 3538948
  395.5 4.0 copy-start.3
  403.2 44.6 %collective-permute-start.6 = (bf16[384,1536]{1,0:T(8,128)(2,1)}, bf16[384,1536]{1,0:T(8,128)(2,1)S(1)}, u32[]{:S(2)}, u32[]{:S(2)}) collective-permute-start(bf16[384,1536]{1,0:T(8,128)(2,1)} %get-tuple-element.160), channel_id=1, source_target_pairs={{0,1},{1,0},{2,3},{3,2},{4,5},{5,4},{6,7},{7,6},{8,9},{9,8},{10,11... | collective-permute-start | bytes 3538952 | tf_op jit(solution)/shard_map/ppermute | solution.py:812
  403.2 44.6 %collective-permute-start.7 = (bf16[384,1536]{1,0:T(8,128)(2,1)}, bf16[384,1536]{1,0:T(8,128)(2,1)}, u32[]{:S(2)}, u32[]{:S(2)}) collective-permute-start(bf16[384,1536]{1,0:T(8,128)(2,1)} %get-tuple-element.161), channel_id=1, source_target_pairs={{0,4},{2,6},{4,0},{6,2},{8,12},{10,14},{12,8},{14,10},{16,20},{18,... | collective-permute-start | bytes 3538952 | tf_op jit(solution)/shard_map/ppermute | solution.py:812
  403.2 44.5 %collective-permute-start.4 = (bf16[384,768]{1,0:T(8,128)(2,1)}, bf16[384,768]{1,0:T(8,128)(2,1)S(1)}, u32[]{:S(2)}, u32[]{:S(2)}) collective-permute-start(bf16[384,768]{1,0:T(8,128)(2,1)} %get-tuple-element.158), channel_id=1, source_target_pairs={{0,4},{2,6},{4,0},{6,2},{8,12},{10,14},{12,8},{14,10},{16,20},{18,... | collective-permute-start | bytes 1769480 | tf_op jit(solution)/shard_map/ppermute | solution.py:812
  405.2 42.5 %collective-permute-start.5 = (bf16[384,768]{1,0:T(8,128)(2,1)}, bf16[384,768]{1,0:T(8,128)(2,1)}, u32[]{:S(2)}, u32[]{:S(2)}) collective-permute-start(bf16[384,768]{1,0:T(8,128)(2,1)} %get-tuple-element.159), channel_id=1, source_target_pairs={{0,1},{1,0},{2,3},{3,2},{4,5},{5,4},{6,7},{7,6},{8,9},{9,8},{10,11... | collective-permute-start | bytes 1769480 | tf_op jit(solution)/shard_map/ppermute | solution.py:812
  447.7 46.5 %copy-start.12 = (bf16[384,768]{1,0:T(8,128)(2,1)}, bf16[384,768]{1,0:T(8,128)(2,1)S(1)}, u32[]{:S(2)}) copy-start(bf16[384,768]{1,0:T(8,128)(2,1)S(1)} %collective-permute-done.4) | copy-start | bytes 1769476
  447.7 63.2 %copy-start.8 = (bf16[384,1536]{1,0:T(8,128)(2,1)}, bf16[384,1536]{1,0:T(8,128)(2,1)S(1)}, u32[]{:S(2)}) copy-start(bf16[384,1536]{1,0:T(8,128)(2,1)S(1)} %collective-permute-done.6) | copy-start | bytes 3538948
  454.1 40.0 %collective-permute-start.8 = (bf16[192,1536]{1,0:T(8,128)(2,1)}, bf16[192,1536]{1,0:T(8,128)(2,1)}, u32[]{:S(2)}, u32[]{:S(2)}) collective-permute-start(bf16[192,1536]{1,0:T(8,128)(2,1)} %pad_maximum_fusion.2), channel_id=1, source_target_pairs={{0,8},{2,10},{4,12},{6,14},{8,0},{10,2},{12,4},{14,6},{16,24},{18,... | collective-permute-start | bytes 1769480 | tf_op jit(solution)/shard_map/ppermute | solution.py:812
  454.1 40.0 %collective-permute-start.9 = (bf16[192,1536]{1,0:T(8,128)(2,1)}, bf16[192,1536]{1,0:T(8,128)(2,1)}, u32[]{:S(2)}, u32[]{:S(2)}) collective-permute-start(bf16[192,1536]{1,0:T(8,128)(2,1)} %get-tuple-element.174), channel_id=1, source_target_pairs={{0,4},{2,6},{4,0},{6,2},{8,12},{10,14},{12,8},{14,10},{16,20},{18,... | collective-permute-start | bytes 1769480 | tf_op jit(solution)/shard_map/ppermute | solution.py:812
  454.1 40.1 %collective-permute-start.10 = (bf16[192,1536]{1,0:T(8,128)(2,1)}, bf16[192,1536]{1,0:T(8,128)(2,1)}, u32[]{:S(2)}, u32[]{:S(2)}) collective-permute-start(bf16[192,1536]{1,0:T(8,128)(2,1)} %get-tuple-element.175), channel_id=1, source_target_pairs={{0,1},{1,0},{2,3},{3,2},{4,5},{5,4},{6,7},{7,6},{8,9},{9,8},{10,11... | collective-permute-start | bytes 1769480 | tf_op jit(solution)/shard_map/ppermute | solution.py:812
  498.3 12.7 %collective-permute-start.11 = (bf16[96,3072]{1,0:T(8,128)(2,1)S(1)}, bf16[96,3072]{1,0:T(8,128)(2,1)S(1)}, u32[]{:S(2)}, u32[]{:S(2)}) collective-permute-start(bf16[96,3072]{1,0:T(8,128)(2,1)S(1)} %pad_maximum_fusion.3), channel_id=1, source_target_pairs={{0,8},{2,10},{4,12},{6,14},{8,0},{10,2},{12,4},{14,6},{16,24},{18,... | collective-permute-start | bytes 1769480 | tf_op jit(solution)/shard_map/ppermute | solution.py:812
  511.0 15.5 %copy-start.13 = (bf16[96,3072]{1,0:T(8,128)(2,1)}, bf16[96,3072]{1,0:T(8,128)(2,1)S(1)}, u32[]{:S(2)}) copy-start(bf16[96,3072]{1,0:T(8,128)(2,1)S(1)} %collective-permute-done.11) | copy-start | bytes 1769476
  513.4 13.1 %copy-start = (bf16[768,1792]{1,0:T(8,128)(2,1)S(1)}, bf16[768,1792]{1,0:T(8,128)(2,1)}, u32[]{:S(2)}) copy-start(bf16[768,1792]{1,0:T(8,128)(2,1)} %get-tuple-element.188.m0) | copy-start | bytes 8257540
  513.4 13.0 %collective-permute-start.12 = (bf16[768,1792]{1,0:T(8,128)(2,1)}, bf16[768,1792]{1,0:T(8,128)(2,1)}, u32[]{:S(2)}, u32[]{:S(2)}) collective-permute-start(bf16[768,1792]{1,0:T(8,128)(2,1)} %get-tuple-element.192), channel_id=1, source_target_pairs={{0,2},{2,0},{4,6},{6,4},{8,10},{10,8},{12,14},{14,12},{16,18},{18,... | collective-permute-start | bytes 8257544 | tf_op jit(solution)/shard_map/ppermute | solution.py:812
  526.5 6.9 %copy-start.1 = (bf16[768,1664]{1,0:T(8,128)(2,1)S(1)}, bf16[768,1664]{1,0:T(8,128)(2,1)}, u32[]{:S(2)}) copy-start(bf16[768,1664]{1,0:T(8,128)(2,1)} %get-tuple-element.197.m1) | copy-start | bytes 7667716
  528.3 5.1 collective-permute-start.14
  528.4 46.7 %collective-permute-start.16 = (bf16[96,1536]{1,0:T(8,128)(2,1)}, bf16[96,1536]{1,0:T(8,128)(2,1)}, u32[]{:S(2)}, u32[]{:S(2)}) collective-permute-start(bf16[96,1536]{1,0:T(8,128)(2,1)} %pad_maximum_fusion.5), channel_id=1, source_target_pairs={{0,16},{2,18},{4,20},{6,22},{8,24},{10,26},{12,28},{14,30},{16,0},... | collective-permute-start | bytes 884744 | tf_op jit(solution)/shard_map/ppermute | solution.py:812
  528.4 46.7 %collective-permute-start.17 = (bf16[48,3072]{1,0:T(8,128)(2,1)}, bf16[48,3072]{1,0:T(8,128)(2,1)}, u32[]{:S(2)}, u32[]{:S(2)}) collective-permute-start(bf16[48,3072]{1,0:T(8,128)(2,1)} %pad_maximum_fusion.6), channel_id=1, source_target_pairs={{0,16},{2,18},{4,20},{6,22},{8,24},{10,26},{12,28},{14,30},{16,0},... | collective-permute-start | bytes 884744 | tf_op jit(solution)/shard_map/ppermute | solution.py:812
  531.4 48.9 %collective-permute-start.13 = (bf16[384,1792]{1,0:T(8,128)(2,1)S(1)}, bf16[384,1792]{1,0:T(8,128)(2,1)S(1)}, u32[]{:S(2)}, u32[]{:S(2)}) collective-permute-start(bf16[384,1792]{1,0:T(8,128)(2,1)S(1)} %add_convert_fusion), channel_id=1, source_target_pairs={{0,1},{1,0},{2,3},{3,2},{4,5},{5,4},{6,7},{7,6},{8,9},{9,8},{10,11... | collective-permute-start | bytes 4128776 | tf_op jit(solution)/shard_map/ppermute | solution.py:812
  533.4 1.5 copy-start.2
  534.8 45.4 %collective-permute-start.15 = (bf16[384,1664]{1,0:T(8,128)(2,1)S(1)}, bf16[384,1664]{1,0:T(8,128)(2,1)}, u32[]{:S(2)}, u32[]{:S(2)}) collective-permute-start(bf16[384,1664]{1,0:T(8,128)(2,1)S(1)} %add_convert_fusion.1), channel_id=1, source_target_pairs={{0,4},{2,6},{4,0},{6,2},{8,12},{10,14},{12,8},{14,10},{16,20},{18,... | collective-permute-start | bytes 3833864 | tf_op jit(solution)/shard_map/ppermute | solution.py:812
  575.1 2.7 copy-start.14
  580.2 1.1 copy-start.5
  581.3 47.8 %copy-start.4 = (bf16[512,1536]{1,0:T(8,128)(2,1)S(1)}, bf16[512,1536]{1,0:T(8,128)(2,1)}, u32[]{:S(2)}) copy-start(bf16[512,1536]{1,0:T(8,128)(2,1)} %get-tuple-element.210) | copy-start | bytes 4718596
  629.2 3.8 copy-start.9
  629.2 3.8 copy-start.10
  629.2 3.8 copy-start.11
Sparse Core Ops, SparseCore 0:
  121.9 80.7 all-gather.1

commit v2 on v1

--- a/solution.py
+++ b/solution.py
@@ -49,9 +49,18 @@
 
 
 H_UNIT = 48
-H_TABLE = 4
 O_UNIT = 32
-O_TABLE = H_TABLE + D // H_UNIT
+
+
+def is_grouped():
+    return D // lax.axis_size(AXES) == H_UNIT
+
+
+def unit_row(unit, size, per_owner):
+    if is_grouped():
+        owner = unit // per_owner
+        unit = kept_at(halving_order(False), owner) * per_owner + (unit - owner * per_owner)
+    return pl.multiple_of(unit * size, 16)
 
 
 def source_chunk(meta, k, slot_chunks):
@@ -103,7 +112,7 @@
                 h_ref[k * Q : (k + 1) * Q, :] = normed.astype(bf16)
                 turned = normed.T.astype(bf16)
                 for n in range(D // H_UNIT):
-                    there = pl.ds(pl.multiple_of(meta[H_TABLE + n], 16), H_UNIT)
+                    there = pl.ds(unit_row(jnp.int32(n), H_UNIT, 1), H_UNIT)
                     ht_ref[there, k * Q : (k + 1) * Q] = turned[n * H_UNIT : (n + 1) * H_UNIT, :]
 
             @pl.when(k >= total)
@@ -276,7 +285,7 @@
             o_ref[:, lanes] = out.astype(bf16)
             turned = out.T.astype(bf16)
             for n in range(128 // O_UNIT):
-                there = pl.ds(pl.multiple_of(meta[O_TABLE + p * (128 // O_UNIT) + n], O_UNIT), O_UNIT)
+                there = pl.ds(unit_row(p * (128 // O_UNIT) + n, O_UNIT, 3), O_UNIT)
                 ot_ref[there, :] = turned[n * O_UNIT : (n + 1) * O_UNIT, :]
             return 0
 
@@ -930,19 +939,30 @@
 
 
 W_COLS = 6528
-W_CUT = 3328
+W_SPANS = ((0, 2944), (2944, 2944), (5888, 640))
 
 
 def gather_kernel(
-    count, inner, flag_ref, shard_ref, tile_ref, tokens_ref, w_ref, tiles_ref, u_ref,
-    kept, given, send_sem, recv_sem, tile_send, tile_recv, own_sem, give_send, give_recv,
+    count, inner, flag_ref, own_ref, norm_ref, conv_ref, bias_ref, inner_ref, tokens_ref,
+    w_ref, wc_ref, g1_ref, g2_ref, u_ref,
+    shard_ref, tile_ref, tiles_ref, kept, given,
+    send_sem, recv_sem, tile_send, tile_recv, own_sem, give_send, give_recv,
 ):
     me = lax.axis_index("dp") * inner + lax.axis_index("fsdp")
     height = shard_ref.shape[0]
     x, core, y = flat_bit("fsdp", 0), flat_bit("dp", 0), flat_bit("dp", 1)
     far = [flat_bit("dp", bit) for bit in range(2, log2(lax.axis_size("dp")))]
-    ways = (far + [y, x, core], far + [x, y, core])
-    spans = (pl.ds(0, W_CUT), pl.ds(W_CUT, W_COLS - W_CUT))
+    ways = (far + [y, x, core], far + [x, y, core], [x, y] + far[::-1] + [core])
+    spans = [pl.ds(at, width) for at, width in W_SPANS]
+    groups = range(len(spans))
+
+    full = PROJ // 128 * 128
+    shard_ref[:, 0:full] = own_ref[:, 0:full].astype(bf16)
+    shard_ref[:, full:] = jnp.zeros((height, W_COLS - full), bf16)
+    shard_ref[:, full:PROJ] = own_ref[:, full:].astype(bf16)
+    tile_ref[...] = jnp.zeros_like(tile_ref)
+    for row, ref in ((0, conv_ref), (4, bias_ref), (5, inner_ref), (6, norm_ref)):
+        tile_ref[row : row + ref.shape[0], 0 : ref.shape[1]] = ref[...].astype(bf16).astype(f32)
 
     def place(away):
         return pl.ds(pl.multiple_of(jnp.bitwise_xor(me, away) * height, height), height)
@@ -1003,14 +1023,12 @@
 
     started = []
     for step in range(len(ways[0])):
-        for half in range(2):
+        for half in groups:
             one = send(half, 0, ways[half][step])
             one.start()
             started.append(one)
     own = pltpu.make_async_copy(shard_ref, w_ref.at[place(0), :], own_sem.at[0])
     own.start()
-    lax.fori_loop(1, count, start_tile, 0)
-    tiles_ref[me] = tile_ref[...]
 
     second = jnp.broadcast_to(flag_ref[0, 0], (1, D)) == 1
     rows = kept.shape[0]
@@ -1023,8 +1041,10 @@
         return 0
 
     lax.fori_loop(0, rows // 64, choose, 0)
-
-    blocks = [(half, away) for half in range(2) for away in range(1, count)]
+    lax.fori_loop(1, count, start_tile, 0)
+    tiles_ref[me] = tile_ref[...]
+
+    blocks = [(half, away) for half in groups for away in range(1, count)]
     blocks.sort(key=lambda b: (b[1].bit_count(), last_step(*b), b[0]))
     tail = []
     for n, (half, away) in enumerate(blocks):
@@ -1043,15 +1063,21 @@
             keep.start()
             give.start()
             tail = [keep, give]
+        if n == 40:
+            lax.fori_loop(1, count, wait_tile, 0)
+            wc_ref[...] = jnp.zeros_like(wc_ref)
+            for owner in range(count):
+                for ref, row, tall in ((wc_ref, 0, 5), (g2_ref, 5, 1), (g1_ref, 6, 1)):
+                    each = ref.shape[1] // count
+                    ref[0:tall, owner * each : (owner + 1) * each] = tiles_ref[owner, row : row + tall, 0:each]
     for one in started:
         one.wait_send()
     for one in tail:
         one.wait()
     own.wait()
-    lax.fori_loop(1, count, wait_tile, 0)
-
-
-def gather(flag, shard, tile, tokens):
+
+
+def gather(flag, own, norm, conv, bias, inner, tokens):
     count = lax.axis_size(AXES)
     slot = tokens.shape[1]
     whole = pl.BlockSpec(memory_space=pltpu.VMEM)
@@ -1061,16 +1087,21 @@
         functools.partial(gather_kernel, count, lax.axis_size("fsdp")),
         out_shape=(
             jax.ShapeDtypeStruct((D, W_COLS), bf16),
-            jax.ShapeDtypeStruct((count, 8, 128), f32),
+            jax.ShapeDtypeStruct((8, XBC), f32),
+            jax.ShapeDtypeStruct((1, D), f32),
+            jax.ShapeDtypeStruct((1, INNER), f32),
             jax.ShapeDtypeStruct((2 * slot, D), bf16),
         ),
-        in_specs=[pl.BlockSpec(memory_space=pltpu.SMEM), whole, whole, whole],
-        out_specs=(anywhere, whole, anywhere),
+        in_specs=[pl.BlockSpec(memory_space=pltpu.SMEM)] + [whole] * 6,
+        out_specs=(anywhere, whole, whole, whole, anywhere),
         scratch_shapes=[
+            pltpu.VMEM((own.shape[0], W_COLS), bf16),
+            pltpu.VMEM((8, 128), f32),
+            pltpu.VMEM((count, 8, 128), f32),
             pltpu.VMEM((slot, D), bf16),
             pltpu.VMEM((slot, D), bf16),
-            dma((2, count)),
-            dma((2, count)),
+            dma((len(W_SPANS), count)),
+            dma((len(W_SPANS), count)),
             dma((count,)),
             dma((count,)),
             dma((2,)),
@@ -1080,7 +1111,7 @@
         compiler_params=params(has_side_effects=True),
         cost_estimate=cost(1e6, 2 * D * W_COLS),
         name="gather",
-    )(flag, shard, tile, tokens)
+    )(flag, own, norm, conv, bias, inner, tokens)
 
 
 def sum_kernel(count, inner, sent_ref, out_ref, came, send_sem, recv_sem):
@@ -1303,45 +1334,32 @@
     cot = cotangent.reshape(rows, D)
     lens = [lengths[first_source], lengths[second_source]]
     chunks = [(n + Q - 1) // Q for n in lens]
-    grouped = D // count == H_UNIT
-    h_units = jnp.arange(D // H_UNIT)
-    o_units = jnp.arange(INNER // O_UNIT)
+    grouped = is_grouped()
+    meta = jnp.stack([chunks[0] + chunks[1], chunks[0], lens[0], lens[1]]).astype(jnp.int32)
+
+    sizes = [v.shape[0] for v in (norm_gain, inner_gain)]
     if grouped:
-        order = halving_order(False)
-        each = INNER // count // O_UNIT
-        h_units = kept_at(order, h_units)
-        o_units = kept_at(order, o_units // each) * each + o_units % each
-    meta = jnp.concatenate(
-        [jnp.stack([chunks[0] + chunks[1], chunks[0], lens[0], lens[1]]), h_units * H_UNIT, o_units * O_UNIT]
-    ).astype(jnp.int32)
-
-    small = [norm_gain, conv_weight.reshape(-1), conv_bias, inner_gain]
-    sizes = [v.shape[0] for v in small]
-    packed = jnp.concatenate(small).astype(bf16)
-    if grouped:
-        tile = jnp.pad(packed.astype(f32), (0, 1024 - packed.shape[0])).reshape(8, 128)
-        shard = jnp.pad(in_weight.astype(bf16), ((0, 0), (0, W_COLS - PROJ)))
-        w1, packed, u = gather(keep_second.astype(jnp.int32).reshape(1, 1), shard, tile, tokens)
-        packed = packed.reshape(count, -1)
+        flag = keep_second.astype(jnp.int32).reshape(1, 1)
+        w1, wc, g1, g2, u = gather(
+            flag, in_weight, norm_gain[None], conv_weight.T, conv_bias[None], inner_gain[None], tokens
+        )
     else:
         outgoing = jnp.where(keep_second, tokens[0], tokens[1])
         incoming = partner(outgoing, "dp", 0)
         u = jnp.concatenate([jnp.where(keep_second, tokens[1], tokens[0]), incoming], axis=0)
         w1 = lax.all_gather(in_weight.astype(bf16), AXES, axis=0, tiled=True)
+        small = [norm_gain, inner_gain, conv_bias, conv_weight.reshape(-1)]
+        packed = jnp.concatenate(small).astype(bf16)
         packed = lax.all_gather(packed[None, :], AXES, axis=0, tiled=True).astype(f32)
-    cuts = [sum(sizes[:n]) for n in range(len(sizes) + 1)]
-    norm_full, conv_full, bias_full, inner_full = (
-        packed[:, cuts[n] : cuts[n + 1]].reshape(-1) for n in range(4)
-    )
+        cuts = [sum(v.shape[0] for v in small[:n]) for n in range(5)]
+        g1, g2, bias, taps = (packed[:, cuts[n] : cuts[n + 1]].reshape(1, -1) for n in range(4))
+        wc = jnp.concatenate([taps.reshape(XBC, CONV).T, bias, jnp.zeros((3, XBC), f32)])
     w2_own, w1 = lax.optimization_barrier([out_weight.astype(bf16), w1])
     w2 = lax.all_gather(w2_own, AXES, axis=0, tiled=True)
 
-    wc = jnp.concatenate([conv_full.reshape(XBC, CONV).T, bias_full[None], jnp.zeros((3, XBC), f32)])
     rate = -jnp.exp(decay_log)
     par = jnp.zeros((8, 128), f32).at[0, :HEADS].set(step_bias).at[1, :HEADS].set(rate)
     skip = jnp.repeat(skip_weight, HEADDIM)[None]
-    g1 = norm_full[None]
-    g2 = inner_full[None]
 
     proj, e, ht = project(meta, u, g1, w1)
     o, ot, y, sin, err = mixer(meta, proj, e, cot, wc, par, skip, g2)
@@ -1382,7 +1400,7 @@
         grad_x, tile, back_half = finish([c_x, c_x1], gconv, gpar, par, gskip, gi, gn, given_half)
         grad_x = [grad_x]
         grad_conv, grad_bias = tile[:CONV, :conv_each].T, tile[CONV, :conv_each]
-        grad_inner, grad_norm = tile[8, : sizes[3]], tile[9, : sizes[0]]
+        grad_inner, grad_norm = tile[8, : sizes[1]], tile[9, : sizes[0]]
         heads = [tile[10 + n, :HEADS] for n in range(3)]
     else:
         back_half = partner(given_half, "dp", 0)

time: 650 us -> 670 us (1.031)
  starting transfers between devices: 7.38 us -> 162 us
  Pallas kernels: 554 us -> 421 us
  local copies, waits for them, and re-layouts: 17 us -> 10.2 us
    ppermute x18, starting transfers between devices: 7.34 us -> 162 us  [partner(): return lax.ppermute(value, axis, pairs)]
    pallas_call x3, Pallas kernels: 137 us -> 85.6 us  [back(): pl.pallas_call(functools.partial(back_kernel, 2, part, parts), out_shape=...]
    pallas_call x1, Pallas kernels: 72.2 us -> 43.9 us  [mixer(): pl.pallas_call(functools.partial(mixer_kernel, 2), out_shape=(jax.ShapeDt...]
    pallas_call x1, Pallas kernels: 55.4 us -> 35.7 us  [gate(): pl.pallas_call(functools.partial(gate_kernel, rows // Q // 2), out_shape=...]
    pallas_call x4, Pallas kernels: 60.3 us -> 44.2 us  [weight_grad(): pl.pallas_call(functools.partial(weight_kernel, rows, swap_from), out_sha...]
    pallas_call x1, Pallas kernels: 40.2 us -> 25.3 us  [input_grad_of(): pl.pallas_call(functools.partial(input_kernel, rows // Q // 2, steps, til...]
    pallas_call x1, Pallas kernels: 42.8 us -> 57.8 us  [finish(): pl.pallas_call(functools.partial(finish_kernel, count, lax.axis_size('fsd...]
    pallas_call x1, Pallas kernels: 37.2 us -> 27.1 us  [project(): pl.pallas_call(functools.partial(project_kernel, rows // Q // 2, steps, t...]
  transfers between devices with their start and end apart: 19 -> 19, of which waited for: 1 -> 3; matrix products, arithmetic and copies ran while one was open for 2% -> 1% of each run, Pallas kernels for 60% -> 38%
where the time goes in v2:
time: 670 us; the launch traced here: 662 us
  Pallas kernels  421 us (63%)
  starting transfers between devices  162 us (24%)
  other arithmetic  40.2 us (6%)
  between operations  20.4 us (3%)
  local copies, waits for them, and re-layouts  10.2 us (2%)
  waiting for transfers between devices  7.7 us (1%)
    ppermute x18, starting transfers between devices, partner(): return lax.ppermute(value, axis, pairs)  162 us
    pallas_call x1, Pallas kernels, gather(): pl.pallas_call(functools.partial(gather_kernel, count, lax.axis_size('fsd...  101 us
    pallas_call x3, Pallas kernels, back(): pl.pallas_call(functools.partial(back_kernel, 2, part, parts), out_shape=...  85.6 us
    pallas_call x1, Pallas kernels, finish(): pl.pallas_call(functools.partial(finish_kernel, count, lax.axis_size('fsd...  57.8 us
    pallas_call x4, Pallas kernels, weight_grad(): pl.pallas_call(functools.partial(weight_kernel, rows, swap_from), out_sha...  44.2 us
    pallas_call x1, Pallas kernels, mixer(): pl.pallas_call(functools.partial(mixer_kernel, 2), out_shape=(jax.ShapeDt...  43.9 us
    pallas_call x1, Pallas kernels, gate(): pl.pallas_call(functools.partial(gate_kernel, rows // Q // 2), out_shape=...  35.7 us
    pallas_call x1, Pallas kernels, project(): pl.pallas_call(functools.partial(project_kernel, rows // Q // 2, steps, t...  27.1 us
  transfers between devices with their start and end apart: 19, of which 3 were waited for; matrix products, arithmetic and copies ran while one was open for 1% of the time, Pallas kernels for 38%

profile of v2, /device:TPU:0, one launch (start us, length us, event | category | flops | bytes accessed | tf_op | source)
XLA Modules:
  0.0 661.6 jit_solution(10160503071095923471)
XLA Ops:
  7.2 0.0 all-gather.2.cloned.1.call-start
  7.2 1.3 fusion.1
  9.2 1.8 convert_element_type.310
  11.0 101.4 %gather.1 = (bf16[1536,6528]{1,0:T(8,128)(2,1)}, f32[8,3328]{1,0:T(8,128)}, f32[1,1536]{1,0:T(1,128)}, f32[1,3072]{1,0:T(1,128)}, bf16[1024,1536]{1,0:T(8,128)(2,1)}) custom-call(s32[1,1]{1,0:T(1,128)} %bitcast.6.flag_ref, f32[48,6448]{1,0:T(8,128)} %own_ref.1, f32[1,48]{1,0:T(1,128)} %bitcast.35, f32[4,104]{1,0:T(4,128)} %bitcast.34, f32[1,104]{1,0:T(1,128)} %bitcast.36, ...), custom_call_target="tpu_custom_call" | custom-call | flops 1000000 | bytes 20054016 | tf_op jit(solution)/shard_map/gather/pallas_call | solution.py:1086
  112.5 0.0 all-gather.2.cloned.1.call-update
  116.4 0.6 fusion
  118.3 0.1 broadcast_in_dim.16
  118.4 0.7 broadcast_in_dim_reshape.3.skip_ref
  119.1 0.2 scatter.9.par_ref
  119.3 1.9 pad_add_fusion.meta
  121.2 27.1 %project.1 = (bf16[1024,6448]{1,0:T(8,128)(2,1)}, f32[1024,128]{1,0:T(8,128)}, bf16[1536,1024]{1,0:T(8,128)(2,1)}) custom-call(s32[4]{0:T(128)} %pad_add_fusion.meta, bf16[1024,1536]{1,0:T(8,128)(2,1)} %get-tuple-element.127.u_ref, f32[1,1536]{1,0:T(1,128)} %get-tuple-element.128.g_ref, bf16[1536,6528]{1,0:T(8,128)(2,1)} %get-tuple-element.130.w_ref), custom_call_target="tpu_custom_call" | custom-call | flops 20283654144 | bytes 33013760 | tf_op jit(solution)/shard_map/project/pallas_call | solution.py:141
  148.3 43.9 %mixer.1 = (bf16[1024,3072]{1,0:T(8,128)(2,1)}, bf16[3072,1024]{1,0:T(8,128)(2,1)}, bf16[1024,3072]{1,0:T(8,128)(2,1)}, bf16[8,128,3072]{2,1,0:T(8,128)(2,1)}, bf16[1024,1536]{1,0:T(8,128)(2,1)}) custom-call(s32[4]{0:T(128)} %pad_add_fusion.meta, bf16[1024,6448]{1,0:T(8,128)(2,1)} %get-tuple-element.131.proj_ref.z_ref.x_ref.prev_ref, ...), custom_call_target="tpu_custom_call" | custom-call | flops 6442450944 | bytes 32079872 | tf_op jit(solution)/shard_map/mixer/pallas_call | solution.py:300
  192.2 12.4 %weight_grad.4 = (bf16[1536,1536]{1,0:T(8,128)(2,1)}, bf16[1536,1536]{1,0:T(8,128)(2,1)}) custom-call(s32[4]{0:T(128)} %pad_add_fusion.meta, bf16[3072,1024]{1,0:T(8,128)(2,1)} %get-tuple-element.135.at_ref, bf16[1024,1536]{1,0:T(8,128)(2,1)} %get-tuple-element.136.b_ref.err_ref), custom_call_target="tpu_custom_call" | custom-call | flops 9663676416 | bytes 18874368 | tf_op jit(solution)/shard_map/weight_grad/pallas_call | solution.py:716
  204.6 57.2 %collective-permute-start = (bf16[1536,1536]{1,0:T(8,128)(2,1)}, bf16[1536,1536]{1,0:T(8,128)(2,1)}, u32[]{:S(2)}, u32[]{:S(2)}) collective-permute-start(bf16[1536,1536]{1,0:T(8,128)(2,1)} %get-tuple-element.144), channel_id=1, source_target_pairs={{0,2},{2,0},{4,6},{6,4},{8,10},{10,8},{12,14},{14,12},{16,18},{18,... | collective-permute-start | bytes 14155784 | tf_op jit(solution)/shard_map/ppermute | solution.py:821
  261.9 35.7 %gate.1 = (bf16[1024,1536]{1,0:T(8,128)(2,1)}, bf16[1024,3072]{1,0:T(8,128)(2,1)}, bf16[1024,3072]{1,0:T(8,128)(2,1)}, f32[1,3072]{1,0:T(1,128)}) custom-call(s32[4]{0:T(128)} %pad_add_fusion.meta, bf16[1024,1536]{1,0:T(8,128)(2,1)} %get-tuple-element.127.u_ref, bf16[1024,1536]{1,0:T(8,128)(2,1)} %get-tuple-element.136.b_ref.err_ref, ...), custom_call_target="tpu_custom_call" | custom-call | flops 19327352832 | bytes 40894464 | tf_op jit(solution)/shard_map/gate/pallas_call | solution.py:415
  297.6 3.9 add_convert_fusion.4
  301.5 12.7 %weight_grad.5 = (bf16[768,3072]{1,0:T(8,128)(2,1)}, bf16[768,3072]{1,0:T(8,128)(2,1)}) custom-call(s32[4]{0:T(128)} %pad_add_fusion.meta, bf16[1536,1024]{1,0:T(8,128)(2,1)} %get-tuple-element.150.at_ref, bf16[1024,3072]{1,0:T(8,128)(2,1)} %get-tuple-element.151.b_ref.dz_ref), custom_call_target="tpu_custom_call" | custom-call | flops 9663676416 | bytes 18874368 | tf_op jit(solution)/shard_map/weight_grad/pallas_call | solution.py:716
  314.2 29.0 %collective-permute-start.3 = (bf16[768,3072]{1,0:T(8,128)(2,1)}, bf16[768,3072]{1,0:T(8,128)(2,1)}, u32[]{:S(2)}, u32[]{:S(2)}) collective-permute-start(bf16[768,3072]{1,0:T(8,128)(2,1)} %get-tuple-element.153), channel_id=1, source_target_pairs={{0,2},{2,0},{4,6},{6,4},{8,10},{10,8},{12,14},{14,12},{16,18},{18,... | collective-permute-start | bytes 14155784 | tf_op jit(solution)/shard_map/ppermute | solution.py:821
  343.2 0.0 collective-permute-start.1
  343.2 39.7 %back.3 = (bf16[1152,3456]{1,0:T(8,128)(2,1)}, f32[8,3328]{1,0:T(8,128)}, f32[8,128]{1,0:T(8,128)}, f32[1,3072]{1,0:T(1,128)}, f32[128,3072]{1,0:T(8,128)}, /*index=5*/f32[8,3328]{1,0:T(8,128)}) custom-call(s32[4]{0:T(128)} %pad_add_fusion.meta, bf16[1024,6448]{1,0:T(8,128)(2,1)} %get-tuple-element.131.proj_ref.z_ref.x_ref.prev_ref, ...), custom_call_target="tpu_custom_call" | custom-call | flops 6039797760 | bytes 12029952 | tf_op jit(solution)/shard_map/back/pallas_call | solution.py:662
  383.0 3.9 add_convert_fusion.8
  386.9 0.1 copy-done.3
  386.9 3.7 add_convert_fusion.2
  390.6 2.2 collective-permute-start.6
  392.8 1.9 collective-permute-start.7
  394.8 0.1 collective-permute-start.4
  394.9 23.1 %back.4 = (bf16[1152,3456]{1,0:T(8,128)(2,1)}, f32[8,3328]{1,0:T(8,128)}, f32[8,128]{1,0:T(8,128)}, f32[1,3072]{1,0:T(1,128)}, f32[128,3072]{1,0:T(8,128)}, /*index=5*/f32[8,3328]{1,0:T(8,128)}) custom-call(s32[4]{0:T(128)} %pad_add_fusion.meta, bf16[1024,6448]{1,0:T(8,128)(2,1)} %get-tuple-element.131.proj_ref.z_ref.x_ref.prev_ref, ...), custom_call_target="tpu_custom_call", output_to_operand_aliasing={{0}: (9, {})} | custom-call | flops 6039797760 | bytes 12029952 | tf_op jit(solution)/shard_map/back/pallas_call | solution.py:662
  418.0 3.5 collective-permute-done.4
  421.5 2.2 add_convert_fusion.13
  423.8 0.9 pad_maximum_fusion.2
  424.7 3.2 add_convert_fusion.6
  427.9 11.7 %collective-permute-start.9 = (bf16[192,1536]{1,0:T(8,128)(2,1)}, bf16[192,1536]{1,0:T(8,128)(2,1)}, u32[]{:S(2)}, u32[]{:S(2)}) collective-permute-start(bf16[192,1536]{1,0:T(8,128)(2,1)} %get-tuple-element.178), channel_id=1, source_target_pairs={{0,4},{2,6},{4,0},{6,2},{8,12},{10,14},{12,8},{14,10},{16,20},{18,... | collective-permute-start | bytes 1769480 | tf_op jit(solution)/shard_map/ppermute | solution.py:821
  439.6 4.1 collective-permute-start.10
  443.7 22.7 %back.5 = (bf16[1152,3456]{1,0:T(8,128)(2,1)}, f32[8,3328]{1,0:T(8,128)}, f32[8,128]{1,0:T(8,128)}, f32[1,3072]{1,0:T(1,128)}) custom-call(s32[4]{0:T(128)} %pad_add_fusion.meta, bf16[1024,6448]{1,0:T(8,128)(2,1)} %get-tuple-element.131.proj_ref.z_ref.x_ref.prev_ref, ...), custom_call_target="tpu_custom_call", output_to_operand_aliasing={{0}: (9, {})} | custom-call | flops 6039797760 | bytes 12029952 | tf_op jit(solution)/shard_map/back/pallas_call | solution.py:662
  466.5 1.5 add_convert_fusion.17
  468.0 0.7 pad_maximum_fusion.5
  468.7 1.8 add_convert_fusion.11
  470.6 1.9 collective-permute-start.11
  472.5 9.3 %weight_grad.6 = (bf16[768,1792]{1,0:T(8,128)(2,1)}, bf16[768,1792]{1,0:T(8,128)(2,1)}) custom-call(s32[4]{0:T(128)} %pad_add_fusion.meta, bf16[1536,1024]{1,0:T(8,128)(2,1)} %get-tuple-element.150.at_ref, bf16[1152,3456]{1,0:T(8,128)(2,1)} %get-tuple-element.191.b_ref.dx_ref), custom_call_target="tpu_custom_call" | custom-call | flops 5637144576 | bytes 12320768 | tf_op jit(solution)/shard_map/weight_grad/pallas_call | solution.py:716
  481.8 2.4 collective-permute-done.11
  484.2 1.7 add_convert_fusion.15
  485.9 0.7 pad_maximum_fusion.6
  486.6 47.6 %collective-permute-start.12 = (bf16[768,1792]{1,0:T(8,128)(2,1)}, bf16[768,1792]{1,0:T(8,128)(2,1)}, u32[]{:S(2)}, u32[]{:S(2)}) collective-permute-start(bf16[768,1792]{1,0:T(8,128)(2,1)} %get-tuple-element.196), channel_id=1, source_target_pairs={{0,2},{2,0},{4,6},{6,4},{8,10},{10,8},{12,14},{14,12},{16,18},{18,... | collective-permute-start | bytes 8257544 | tf_op jit(solution)/shard_map/ppermute | solution.py:821
  534.2 9.7 %weight_grad.7 = (bf16[768,1664]{1,0:T(8,128)(2,1)}, bf16[768,1664]{1,0:T(8,128)(2,1)}) custom-call(s32[4]{0:T(128)} %pad_add_fusion.meta, bf16[1536,1024]{1,0:T(8,128)(2,1)} %get-tuple-element.150.at_ref, bf16[1152,3456]{1,0:T(8,128)(2,1)} %get-tuple-element.191.b_ref.dx_ref), custom_call_target="tpu_custom_call" | custom-call | flops 5234491392 | bytes 11665408 | tf_op jit(solution)/shard_map/weight_grad/pallas_call | solution.py:716
  544.0 1.8 add_convert_fusion
  545.8 3.5 collective-permute-start.14
  549.3 2.9 collective-permute-start.17
  552.2 1.7 collective-permute-done.14.a1
  553.9 0.3 add_convert_fusion.1
  554.2 1.1 copy-done.2
  555.4 25.3 %input_grad.1 = (bf16[512,1536]{1,0:T(8,128)(2,1)}, bf16[512,1536]{1,0:T(8,128)(2,1)}, f32[1,1536]{1,0:T(1,128)}) custom-call(s32[4]{0:T(128)} %pad_add_fusion.meta, bf16[1024,1536]{1,0:T(8,128)(2,1)} %get-tuple-element.127.u_ref, bf16[1024,1536]{1,0:T(8,128)(2,1)} %get-tuple-element.136.b_ref.err_ref, f32[1,1536]{1,0:T(1,128)} %get-tuple-element.128.g_ref, ...), custom_call_target="tpu_custom_call" | custom-call | flops 20283654144 | bytes 33013760 | tf_op jit(solution)/shard_map/input_grad/pallas_call | solution.py:787
  580.7 0.0 copy-start.14
  580.7 1.8 convert_add_fusion.1
  582.5 0.9 pad_maximum_fusion.4
  583.4 2.5 convert_add_fusion.3
  585.8 0.0 collective-permute-done.15.b1
  585.9 1.1 copy-done.5
  586.9 57.8 %finish.1 = (f32[48,3456]{1,0:T(8,128)}, f32[16,128]{1,0:T(8,128)}, bf16[512,1536]{1,0:T(8,128)(2,1)}) custom-call(bf16[768,1792]{1,0:T(8,128)(2,1)} %get-tuple-element.192.m0, bf16[768,1792]{1,0:T(8,128)(2,1)} %collective-permute-done.12.a0, bf16[384,1792]{1,0:T(8,128)(2,1)} %copy-done.5, bf16[768,1664]{1,0:T(8,128)(2,1)} %get-tuple-element.201.m1, ...), custom_call_target="tpu_custom_call" | custom-call | flops 10000000 | bytes 20000000 | tf_op jit(solution)/shard_map/finish/pallas_call | solution.py:1294
  644.7 1.4 slice_bitcast_fusion.2
  646.0 1.2 slice_bitcast_fusion
  647.3 1.2 slice_bitcast_fusion.5
  648.5 1.2 slice_bitcast_fusion.1
  649.7 3.8 maximum_select_fusion
  653.5 1.1 pad_maximum_fusion
  (60 shorter events, 0.2 us)
Async XLA Ops:
  7.2 254.7 %all-gather.2.cloned.1.call-start = ((), (), s32[]{:S(2)}) async-start(), calls=%async_computation | async-start | bytes 9732096 | tf_op jit(solution)/shard_map/all_gather | solution.py:1358
  11.0 105.4 %copy-start.16 = (s32[64]{0:T(128)S(1)}, s32[64]{0:T(128)}, u32[]{:S(2)}) copy-start(s32[64]{0:T(128)} %param.19) | copy-start | bytes 772
  11.0 107.3 %copy-start.17 = (f32[48]{0:T(128)S(1)}, f32[48]{0:T(128)}, u32[]{:S(2)}) copy-start(f32[48]{0:T(128)} %param.27) | copy-start | bytes 580
  11.0 108.1 %copy-start.18 = (f32[48]{0:T(128)S(1)}, f32[48]{0:T(128)}, u32[]{:S(2)}) copy-start(f32[48]{0:T(128)} %param.25) | copy-start | bytes 580
  11.0 108.1 %copy-start.19 = (f32[48]{0:T(128)S(1)}, f32[48]{0:T(128)}, u32[]{:S(2)}) copy-start(f32[48]{0:T(128)} %param.26) | copy-start | bytes 580
  119.3 29.0 %copy-start.15 = (f32[8,128]{1,0:T(8,128)}, f32[8,128]{1,0:T(8,128)S(1)}, u32[]{:S(2)}) copy-start(f32[8,128]{1,0:T(8,128)S(1)} %scatter.9.par_ref) | copy-start | bytes 12292
  204.6 92.9 %collective-permute-start = (bf16[1536,1536]{1,0:T(8,128)(2,1)}, bf16[1536,1536]{1,0:T(8,128)(2,1)}, u32[]{:S(2)}, u32[]{:S(2)}) collective-permute-start(bf16[1536,1536]{1,0:T(8,128)(2,1)} %get-tuple-element.144), channel_id=1, source_target_pairs={{0,2},{2,0},{4,6},{6,4},{8,10},{10,8},{12,14},{14,12},{16,18},{18,... | collective-permute-start | bytes 14155784 | tf_op jit(solution)/shard_map/ppermute | solution.py:821
  314.2 68.8 %collective-permute-start.3 = (bf16[768,3072]{1,0:T(8,128)(2,1)}, bf16[768,3072]{1,0:T(8,128)(2,1)}, u32[]{:S(2)}, u32[]{:S(2)}) collective-permute-start(bf16[768,3072]{1,0:T(8,128)(2,1)} %get-tuple-element.153), channel_id=1, source_target_pairs={{0,2},{2,0},{4,6},{6,4},{8,10},{10,8},{12,14},{14,12},{16,18},{18,... | collective-permute-start | bytes 14155784 | tf_op jit(solution)/shard_map/ppermute | solution.py:821
  343.2 39.7 %collective-permute-start.1 = (bf16[768,768]{1,0:T(8,128)(2,1)}, bf16[768,768]{1,0:T(8,128)(2,1)S(1)}, u32[]{:S(2)}, u32[]{:S(2)}) collective-permute-start(bf16[768,768]{1,0:T(8,128)(2,1)} %get-tuple-element.147), channel_id=1, source_target_pairs={{0,1},{1,0},{2,3},{3,2},{4,5},{5,4},{6,7},{7,6},{8,9},{9,8},{10,11... | collective-permute-start | bytes 3538952 | tf_op jit(solution)/shard_map/ppermute | solution.py:821
  343.2 39.7 %collective-permute-start.2 = (bf16[768,768]{1,0:T(8,128)(2,1)S(1)}, bf16[768,768]{1,0:T(8,128)(2,1)S(1)}, u32[]{:S(2)}, u32[]{:S(2)}) collective-permute-start(bf16[768,768]{1,0:T(8,128)(2,1)S(1)} %get-tuple-element.148), channel_id=1, source_target_pairs={{0,4},{2,6},{4,0},{6,2},{8,12},{10,14},{12,8},{14,10},{16,20},{18,... | collective-permute-start | bytes 3538952 | tf_op jit(solution)/shard_map/ppermute | solution.py:821
  382.9 83.6 %copy-start.6 = (bf16[768,768]{1,0:T(8,128)(2,1)}, bf16[768,768]{1,0:T(8,128)(2,1)S(1)}, u32[]{:S(2)}) copy-start(bf16[768,768]{1,0:T(8,128)(2,1)S(1)} %collective-permute-done.1) | copy-start | bytes 3538948
  382.9 83.6 %copy-start.7 = (bf16[768,768]{1,0:T(8,128)(2,1)}, bf16[768,768]{1,0:T(8,128)(2,1)S(1)}, u32[]{:S(2)}) copy-start(bf16[768,768]{1,0:T(8,128)(2,1)S(1)} %collective-permute-done.2) | copy-start | bytes 3538948
  382.9 4.0 copy-start.3
  390.6 30.9 %collective-permute-start.6 = (bf16[384,1536]{1,0:T(8,128)(2,1)}, bf16[384,1536]{1,0:T(8,128)(2,1)S(1)}, u32[]{:S(2)}, u32[]{:S(2)}) collective-permute-start(bf16[384,1536]{1,0:T(8,128)(2,1)} %get-tuple-element.164), channel_id=1, source_target_pairs={{0,1},{1,0},{2,3},{3,2},{4,5},{5,4},{6,7},{7,6},{8,9},{9,8},{10,11... | collective-permute-start | bytes 3538952 | tf_op jit(solution)/shard_map/ppermute | solution.py:821
  392.8 28.7 %collective-permute-start.7 = (bf16[384,1536]{1,0:T(8,128)(2,1)}, bf16[384,1536]{1,0:T(8,128)(2,1)}, u32[]{:S(2)}, u32[]{:S(2)}) collective-permute-start(bf16[384,1536]{1,0:T(8,128)(2,1)} %get-tuple-element.165), channel_id=1, source_target_pairs={{0,4},{2,6},{4,0},{6,2},{8,12},{10,14},{12,8},{14,10},{16,20},{18,... | collective-permute-start | bytes 3538952 | tf_op jit(solution)/shard_map/ppermute | solution.py:821
  394.8 26.7 %collective-permute-start.4 = (bf16[384,768]{1,0:T(8,128)(2,1)}, bf16[384,768]{1,0:T(8,128)(2,1)S(1)}, u32[]{:S(2)}, u32[]{:S(2)}) collective-permute-start(bf16[384,768]{1,0:T(8,128)(2,1)} %get-tuple-element.162), channel_id=1, source_target_pairs={{0,4},{2,6},{4,0},{6,2},{8,12},{10,14},{12,8},{14,10},{16,20},{18,... | collective-permute-start | bytes 1769480 | tf_op jit(solution)/shard_map/ppermute | solution.py:821
  394.8 26.7 %collective-permute-start.5 = (bf16[384,768]{1,0:T(8,128)(2,1)}, bf16[384,768]{1,0:T(8,128)(2,1)}, u32[]{:S(2)}, u32[]{:S(2)}) collective-permute-start(bf16[384,768]{1,0:T(8,128)(2,1)} %get-tuple-element.163), channel_id=1, source_target_pairs={{0,1},{1,0},{2,3},{3,2},{4,5},{5,4},{6,7},{7,6},{8,9},{9,8},{10,11... | collective-permute-start | bytes 1769480 | tf_op jit(solution)/shard_map/ppermute | solution.py:821
  421.5 45.0 %copy-start.12 = (bf16[384,768]{1,0:T(8,128)(2,1)}, bf16[384,768]{1,0:T(8,128)(2,1)S(1)}, u32[]{:S(2)}) copy-start(bf16[384,768]{1,0:T(8,128)(2,1)S(1)} %collective-permute-done.4) | copy-start | bytes 1769476
  421.5 62.7 %copy-start.8 = (bf16[384,1536]{1,0:T(8,128)(2,1)}, bf16[384,1536]{1,0:T(8,128)(2,1)S(1)}, u32[]{:S(2)}) copy-start(bf16[384,1536]{1,0:T(8,128)(2,1)S(1)} %collective-permute-done.6) | copy-start | bytes 3538948
  427.9 38.6 %collective-permute-start.8 = (bf16[192,1536]{1,0:T(8,128)(2,1)}, bf16[192,1536]{1,0:T(8,128)(2,1)}, u32[]{:S(2)}, u32[]{:S(2)}) collective-permute-start(bf16[192,1536]{1,0:T(8,128)(2,1)} %pad_maximum_fusion.2), channel_id=1, source_target_pairs={{0,8},{2,10},{4,12},{6,14},{8,0},{10,2},{12,4},{14,6},{16,24},{18,... | collective-permute-start | bytes 1769480 | tf_op jit(solution)/shard_map/ppermute | solution.py:821
  427.9 38.6 %collective-permute-start.9 = (bf16[192,1536]{1,0:T(8,128)(2,1)}, bf16[192,1536]{1,0:T(8,128)(2,1)}, u32[]{:S(2)}, u32[]{:S(2)}) collective-permute-start(bf16[192,1536]{1,0:T(8,128)(2,1)} %get-tuple-element.178), channel_id=1, source_target_pairs={{0,4},{2,6},{4,0},{6,2},{8,12},{10,14},{12,8},{14,10},{16,20},{18,... | collective-permute-start | bytes 1769480 | tf_op jit(solution)/shard_map/ppermute | solution.py:821
  439.6 26.9 %collective-permute-start.10 = (bf16[192,1536]{1,0:T(8,128)(2,1)}, bf16[192,1536]{1,0:T(8,128)(2,1)}, u32[]{:S(2)}, u32[]{:S(2)}) collective-permute-start(bf16[192,1536]{1,0:T(8,128)(2,1)} %get-tuple-element.179), channel_id=1, source_target_pairs={{0,1},{1,0},{2,3},{3,2},{4,5},{5,4},{6,7},{7,6},{8,9},{9,8},{10,11... | collective-permute-start | bytes 1769480 | tf_op jit(solution)/shard_map/ppermute | solution.py:821
  470.6 13.6 %collective-permute-start.11 = (bf16[96,3072]{1,0:T(8,128)(2,1)S(1)}, bf16[96,3072]{1,0:T(8,128)(2,1)S(1)}, u32[]{:S(2)}, u32[]{:S(2)}) collective-permute-start(bf16[96,3072]{1,0:T(8,128)(2,1)S(1)} %pad_maximum_fusion.3), channel_id=1, source_target_pairs={{0,8},{2,10},{4,12},{6,14},{8,0},{10,2},{12,4},{14,6},{16,24},{18,... | collective-permute-start | bytes 1769480 | tf_op jit(solution)/shard_map/ppermute | solution.py:821
  484.2 59.8 %copy-start.13 = (bf16[96,3072]{1,0:T(8,128)(2,1)}, bf16[96,3072]{1,0:T(8,128)(2,1)S(1)}, u32[]{:S(2)}) copy-start(bf16[96,3072]{1,0:T(8,128)(2,1)S(1)} %collective-permute-done.11) | copy-start | bytes 1769476
  486.6 57.4 %copy-start = (bf16[768,1792]{1,0:T(8,128)(2,1)S(1)}, bf16[768,1792]{1,0:T(8,128)(2,1)}, u32[]{:S(2)}) copy-start(bf16[768,1792]{1,0:T(8,128)(2,1)} %get-tuple-element.192.m0) | copy-start | bytes 8257540
  486.6 57.4 %collective-permute-start.12 = (bf16[768,1792]{1,0:T(8,128)(2,1)}, bf16[768,1792]{1,0:T(8,128)(2,1)}, u32[]{:S(2)}, u32[]{:S(2)}) collective-permute-start(bf16[768,1792]{1,0:T(8,128)(2,1)} %get-tuple-element.196), channel_id=1, source_target_pairs={{0,2},{2,0},{4,6},{6,4},{8,10},{10,8},{12,14},{14,12},{16,18},{18,... | collective-permute-start | bytes 8257544 | tf_op jit(solution)/shard_map/ppermute | solution.py:821
  544.0 9.9 %copy-start.1 = (bf16[768,1664]{1,0:T(8,128)(2,1)S(1)}, bf16[768,1664]{1,0:T(8,128)(2,1)}, u32[]{:S(2)}) copy-start(bf16[768,1664]{1,0:T(8,128)(2,1)} %get-tuple-element.201.m1) | copy-start | bytes 7667716
  545.8 8.1 %collective-permute-start.14 = (bf16[768,1664]{1,0:T(8,128)(2,1)}, bf16[768,1664]{1,0:T(8,128)(2,1)S(1)}, u32[]{:S(2)}, u32[]{:S(2)}) collective-permute-start(bf16[768,1664]{1,0:T(8,128)(2,1)} %get-tuple-element.202), channel_id=1, source_target_pairs={{0,2},{2,0},{4,6},{6,4},{8,10},{10,8},{12,14},{14,12},{16,18},{18,... | collective-permute-start | bytes 7667720 | tf_op jit(solution)/shard_map/ppermute | solution.py:821
  549.3 31.4 %collective-permute-start.16 = (bf16[96,1536]{1,0:T(8,128)(2,1)}, bf16[96,1536]{1,0:T(8,128)(2,1)}, u32[]{:S(2)}, u32[]{:S(2)}) collective-permute-start(bf16[96,1536]{1,0:T(8,128)(2,1)} %pad_maximum_fusion.5), channel_id=1, source_target_pairs={{0,16},{2,18},{4,20},{6,22},{8,24},{10,26},{12,28},{14,30},{16,0},... | collective-permute-start | bytes 884744 | tf_op jit(solution)/shard_map/ppermute | solution.py:821
  549.3 31.4 %collective-permute-start.17 = (bf16[48,3072]{1,0:T(8,128)(2,1)}, bf16[48,3072]{1,0:T(8,128)(2,1)}, u32[]{:S(2)}, u32[]{:S(2)}) collective-permute-start(bf16[48,3072]{1,0:T(8,128)(2,1)} %pad_maximum_fusion.6), channel_id=1, source_target_pairs={{0,16},{2,18},{4,20},{6,22},{8,24},{10,26},{12,28},{14,30},{16,0},... | collective-permute-start | bytes 884744 | tf_op jit(solution)/shard_map/ppermute | solution.py:821
  552.2 33.6 %collective-permute-start.13 = (bf16[384,1792]{1,0:T(8,128)(2,1)S(1)}, bf16[384,1792]{1,0:T(8,128)(2,1)S(1)}, u32[]{:S(2)}, u32[]{:S(2)}) collective-permute-start(bf16[384,1792]{1,0:T(8,128)(2,1)S(1)} %add_convert_fusion), channel_id=1, source_target_pairs={{0,1},{1,0},{2,3},{3,2},{4,5},{5,4},{6,7},{7,6},{8,9},{9,8},{10,11... | collective-permute-start | bytes 4128776 | tf_op jit(solution)/shard_map/ppermute | solution.py:821
  553.9 1.5 copy-start.2
  555.4 30.5 %collective-permute-start.15 = (bf16[384,1664]{1,0:T(8,128)(2,1)S(1)}, bf16[384,1664]{1,0:T(8,128)(2,1)}, u32[]{:S(2)}, u32[]{:S(2)}) collective-permute-start(bf16[384,1664]{1,0:T(8,128)(2,1)S(1)} %add_convert_fusion.1), channel_id=1, source_target_pairs={{0,4},{2,6},{4,0},{6,2},{8,12},{10,14},{12,8},{14,10},{16,20},{18,... | collective-permute-start | bytes 3833864 | tf_op jit(solution)/shard_map/ppermute | solution.py:821
  580.7 2.7 copy-start.14
  585.8 1.1 copy-start.5
  586.9 62.7 %copy-start.4 = (bf16[512,1536]{1,0:T(8,128)(2,1)S(1)}, bf16[512,1536]{1,0:T(8,128)(2,1)}, u32[]{:S(2)}) copy-start(bf16[512,1536]{1,0:T(8,128)(2,1)} %get-tuple-element.214) | copy-start | bytes 4718596
  649.6 3.8 copy-start.9
  649.6 3.8 copy-start.10
  649.6 3.8 copy-start.11
Sparse Core Ops, SparseCore 0:
  112.6 80.2 all-gather.1
